TPU v7x, 128 devices: a whole 4x4x4 slice. The times are simulated.
128 devices in a mesh: dp: 4 (over y), fsdp: 4 (over x_lo, core), ctx: 8 (over z, x_hi).
Axes of the slice: x: 4 (x_hi: 2, x_lo: 2; x = x_hi * 2 + x_lo), y: 4, z: 4, core: 2. Of those that a mesh axis runs over, the one named last changes fastest.
Arguments:
- tokens: bfloat16 [16, 4096, 1024], P(('dp', 'fsdp'), 'ctx')
- bounds: int32 [16, 4096], P(('dp', 'fsdp'), 'ctx'), may hold values 0 or 1
- decay_rates: float32 [16], replicated, may hold values from 2.4414063e-05 to 0.9
- w_query: bfloat16 [1024, 1024], P('fsdp')
- w_key: bfloat16 [1024, 1024], P('fsdp')
- w_up: bfloat16 [1024, 2048], P('fsdp'), may hold values from -0.1875 to 0.1875
- grad_out: bfloat16 [16, 4096, 2048], P(('dp', 'fsdp'), 'ctx'), may hold values from -6 to 6
Outputs:
- dechunked: bfloat16 [16, 4096, 2048], P(('dp', 'fsdp'), 'ctx')
- grad_tokens: bfloat16 [16, 4096, 1024], P(('dp', 'fsdp'), 'ctx')
- grad_query: float32 [1024, 1024], P('fsdp')
- grad_key: float32 [1024, 1024], P('fsdp')
- grad_up: float32 [1024, 2048], P('fsdp')
All inputs are finite; a program needn't handle non-finite values. No bound on the sum of `bounds` on one device may be relied on, other than what follows from the above.
Results may differ from a plain program's by a relative error of at most 0.0049.
Values may be sent and summed in bfloat16 or wider, within the bound.
No kernel may reach another device: no remote copies, remote signals or barrier semaphores. Data moves between devices by JAX's collectives and lax.ppermute only.
A program may use at most 128 MiB of HBM per device.

v0:
```python
import functools

import jax
import jax.numpy as jnp
from jax import lax
from jax.experimental import pallas as pl
from jax.experimental.pallas import tpu as pltpu
from jax.sharding import PartitionSpec as P


SPAN = 128
LANES = 128
epsilon = 1e-06
CTX = ("z", "xh")
RANGES = 8
HIGHEST = lax.Precision.HIGHEST
F32 = jnp.float32
BF16 = jnp.bfloat16


def along_x(a, by):
    pairs = []
    for xl in range(2):
        for xh in range(2):
            x = (xh * 2 + xl + by) % 4
            pairs.append((xl * 2 + xh, (x % 2) * 2 + x // 2))
    return lax.ppermute(a, ("xl", "xh"), pairs)


def swap_core(a):
    return lax.ppermute(a, "core", [(0, 1), (1, 0)])


def along_ctx(a, by):
    return lax.ppermute(
        a, CTX, [(i, i + by) for i in range(RANGES) if 0 <= i + by < RANGES]
    )


def mxu(a, b):
    return jnp.dot(a, b, preferred_element_type=F32)


def halves(a):
    high = a.astype(BF16)
    return high, (a - high.astype(F32)).astype(BF16)


def ids(shape, dim):
    return lax.broadcasted_iota(jnp.int32, shape, dim)


def head_cols(h):
    return slice(h * LANES, (h + 1) * LANES)


def span(n):
    return pl.ds(pl.multiple_of(n * SPAN, SPAN), SPAN)


def fetch_panel(place, pieces, whole, sems):
    core = place[0] % 2
    split = len(pieces) // 2
    rows = whole.shape[0] // 2
    copies = []
    for j, piece in enumerate(pieces):
        part = piece.shape[0]
        start = (core ^ (j // split)) * rows + (j % split) * part
        copies.append(
            pltpu.make_async_copy(
                piece, whole.at[pl.ds(pl.multiple_of(start, part), part), :], sems.at[j]
            )
        )
    return copies


def block_copy(source, target, sems, n):
    return pltpu.make_async_copy(source.at[span(n), :], target.at[span(n), :], sems.at[n])


def whole_copy(source, target, sem):
    return pltpu.make_async_copy(source, target, sem)


def panel_columns(index, depth):
    return pl.ds(pl.multiple_of(index * depth, depth), depth)


def near_kernel(place, tok, q0, q1, queries, turned, wq, q_sems):
    loads = fetch_panel(place, (q0, q1), wq, q_sems)
    for c in loads:
        c.start()
    turned[...] = tok[...].T
    for c in loads:
        c.wait()
    queries[...] = mxu(tok[:, panel_columns(place[0] // 2, wq.shape[0])], wq[...])


def near_values_kernel(
    place, tok, tok_prev, u0, u1, u2, u3, values, turned_prev, wu, sems
):
    loads = fetch_panel(place, (u0, u1, u2, u3), wu, sems)
    for c in loads:
        c.start()
    turned_prev[...] = tok_prev[...].T
    for c in loads:
        c.wait()
    values[...] = mxu(tok[:, panel_columns(place[0] // 2, wu.shape[0])], wu[...])


def rates_kernel(
    place, bounds, decay, tok, tok_prev, cot, q_part, q2, q3, k0, k1, k2, k3,
    queries, keys, adjoint, mix_out, keep_out, stats_out, outs, carry,
    wq, wk, q_sems, k_sems,
):
    hidden = adjoint.shape[1]
    heads = hidden // LANES
    blocks = adjoint.shape[0] // SPAN
    load_q = fetch_panel(place, (q2, q3), wq, q_sems)
    side, depth = place[0] // 2, wq.shape[0]
    load_k = []
    for i, pieces in enumerate(((k0, k1), (k2, k3))):
        rows = panel_columns(side + i * (1 - 2 * side), depth)
        load_k += fetch_panel(place, pieces, wk.at[rows, :], k_sems.at[i])
    for c in load_q + load_k:
        c.start()
    carry[0:1, :] = jnp.zeros((1, hidden), F32)
    carry[1:2, :] = jnp.ones((1, hidden), F32)
    cols = panel_columns(1 - side, depth)
    for c in load_q:
        c.wait()
    queries[...] = q_part[...] + mxu(tok[:, cols], wq[...])
    for c in load_k:
        c.wait()
    keys[...] = mxu(tok_prev[...], wk[...])

    @pl.loop(0, blocks)
    def _(step):
        n = blocks - 1 - step
        rows = span(n)
        q, k = queries[rows, :], keys[rows, :]
        iq = lax.rsqrt(jnp.sum(q * q, -1, keepdims=True) + epsilon)
        ik = lax.rsqrt(jnp.sum(k * k, -1, keepdims=True) + epsilon)
        cosine = jnp.sum(q * k, -1, keepdims=True) * iq * ik
        lane = ids((SPAN, LANES), 1)
        sub = ids((SPAN, LANES), 0)
        first = jnp.logical_and(place[1] + place[2] == 0, n == 0)
        opening = jnp.logical_and(first, ids((SPAN, 1), 0) == 0)
        prob = jnp.where(opening, 1.0, 0.5 * (1.0 - cosine))
        marks = jnp.broadcast_to(bounds[:, rows].astype(F32), (SPAN, SPAN)).T[:, 0:1]
        marked = jnp.where(opening, 1.0, marks)
        mix = (marked * prob) * decay[...]
        logs = jnp.log(1.0 - mix)
        lower = (sub >= lane).astype(F32)
        keep = jnp.dot(lower, logs, precision=HIGHEST, preferred_element_type=F32)
        keep_rows = keep.T
        active = jnp.where(opening, 0.0, marked)
        stats = jnp.where(
            lane == 0, iq, jnp.where(lane == 1, ik, jnp.where(lane == 2, cosine, active))
        )
        mix_out[rows, :] = mix
        keep_out[rows, :] = keep
        stats_out[rows, :] = stats
        outs[pl.ds(n, 1), :] = carry[0:1, :]
        total = jnp.exp(keep[SPAN - 1 : SPAN, :])
        upper = sub <= lane
        for h in range(heads):
            cols = head_cols(h)
            gap = keep_rows[h : h + 1, :] - keep[:, h : h + 1]
            band = jnp.where(upper, jnp.exp(jnp.where(upper, gap, 0.0)), 0.0)
            local = mxu(band.astype(BF16), cot[rows, cols])
            adjoint[rows, cols] = local
            d = total[:, h : h + 1]
            carry[0:1, cols] = d * carry[0:1, cols] + (1.0 - mix[0:1, h : h + 1]) * local[0:1, :]
            carry[1:2, cols] = d * carry[1:2, cols]


def states_kernel(
    place, mix_ref, keep_ref, tok, b_carry, v_part, u4, u5, u6, u7,
    values, states, ins, message,
    wu, carry, u_sems,
):
    hidden = values.shape[1]
    heads = hidden // LANES
    blocks = values.shape[0] // SPAN
    loads = fetch_panel(place, (u4, u5, u6, u7), wu, u_sems)
    for c in loads:
        c.start()
    carry[...] = jnp.zeros_like(carry)
    message[0:2, :] = b_carry[...]
    cols = panel_columns(1 - place[0] // 2, wu.shape[0])
    for c in loads:
        c.wait()
    values[...] = v_part[...] + mxu(tok[:, cols], wu[...])

    @pl.loop(0, blocks)
    def _(n):
        rows = span(n)
        mix, keep = mix_ref[rows, :], keep_ref[rows, :]
        keep_rows = keep.T
        lower = ids((SPAN, LANES), 0) >= ids((SPAN, LANES), 1)
        ins[pl.ds(n, 1), :] = carry[0:1, :]
        total = jnp.exp(keep[SPAN - 1 : SPAN, :])
        for h in range(heads):
            cols = head_cols(h)
            gap = keep[:, h : h + 1] - keep_rows[h : h + 1, :]
            band = jnp.where(lower, jnp.exp(jnp.where(lower, gap, 0.0)), 0.0)
            band = band.astype(BF16)
            added, rest = halves(mix[:, h : h + 1] * values[rows, cols])
            local = mxu(band, added) + mxu(band, rest)
            states[rows, cols] = local
            carry[0:1, cols] = total[:, h : h + 1] * carry[0:1, cols] + local[SPAN - 1 : SPAN, :]

    message[2:3, :] = carry[...]


def chain(own, message, incoming, row):
    return jnp.where(own, message[1:2, :] * incoming + message[row : row + 1, :], incoming)


def pair_kernel(place, message, other, pair):
    low = jnp.where(place[2] == 0, message[...], other[...])
    high = jnp.where(place[2] == 0, other[...], message[...])
    pair[0:1, :] = low[1:2] * high[0:1] + low[0:1]
    pair[1:2, :] = low[1:2] * high[1:2]
    pair[2:3, :] = high[1:2] * low[2:3] + high[2:3]


def adjoint_in(place, other, after):
    incoming = jnp.zeros((1, other.shape[1]), F32)
    for d in (3, 2, 1):
        incoming = chain(place[1] + d <= 3, after[d - 1], incoming, 0)
    return chain(place[2] == 0, other, incoming, 0)


def state_in(place, other, after):
    incoming = jnp.zeros((1, other.shape[1]), F32)
    for d in (3, 2, 1):
        incoming = chain(place[1] - d >= 0, after[3 - d], incoming, 2)
    return chain(place[2] == 1, other, incoming, 2)


def side_rows(core, turned, b):
    rows = turned.shape[0] // 4
    return turned[pl.ds(pl.multiple_of((2 * b + core) * rows, rows), rows), :]


def shares(core, turned, d, share, share_out, sems):
    step = 512
    saves = []
    rows = share.shape[0] // 2
    for i in range(d.shape[1] // step):
        part = slice(i * step, (i + 1) * step)
        for b in range(2):
            share[b * rows : (b + 1) * rows, part] = mxu(
                side_rows(core, turned, b), d[:, part]
            ).astype(BF16)
        saves.append(whole_copy(share.at[:, part], share_out.at[:, part], sems.at[i]))
        saves[i].start()
    return saves


def adjoint_kernel(
    place, outs, mix_ref, keep_ref, other, next1, next2, next3, local, turned,
    d_values, tails, share_out, share, s_sems,
):
    heads = local.shape[1] // LANES
    blocks = local.shape[0] // SPAN
    incoming = adjoint_in(place, other, (next1, next2, next3))

    def block(step, after):
        n = blocks - 1 - step
        rows = span(n)
        mix, keep = mix_ref[rows, :], keep_ref[rows, :]
        last = keep[SPAN - 1 : SPAN, :]
        fade = jnp.exp(last - keep)
        reach = jnp.exp(after)
        back = outs[pl.ds(n, 1), :]
        ends = []
        for h in range(heads):
            cols = head_cols(h)
            tail = back[:, cols] + reach[:, h : h + 1] * incoming[:, cols]
            ends.append(tail)
            full = local[rows, cols] + fade[:, h : h + 1] * tail
            d_values[rows, cols] = (mix[:, h : h + 1] * full).astype(BF16)
        tails[pl.ds(n, 1), :] = jnp.concatenate(ends, 1)
        return after + last

    lax.fori_loop(0, blocks, block, jnp.zeros((1, LANES), F32))
    saves = shares(1 - place[0] % 2, turned, d_values, share, share_out, s_sems)
    for c in saves:
        c.wait()


def router_kernel(
    place, ins, tails, keep_ref, stats_ref, decay, other, next1, next2, next3,
    local, values, adjoint, queries, keys,
    d_query, d_prev, dechunked_out, dechunked, d_sems,
):
    heads = values.shape[1] // LANES
    blocks = values.shape[0] // SPAN
    incoming = state_in(place, other, (next1, next2, next3))

    def block(n, before):
        rows = span(n)
        keep = keep_ref[rows, :]
        fade = jnp.exp(keep)
        last = keep[SPAN - 1 : SPAN, :]
        fade_back = jnp.exp(last - keep)
        reach = jnp.exp(before)
        start = ins[pl.ds(n, 1), :]
        tail = tails[pl.ds(n, 1), :]
        top = ids((SPAN, LANES), 0) == 0
        total = jnp.zeros((SPAN, LANES), F32)
        for h in range(heads):
            cols = head_cols(h)
            base = start[:, cols] + reach[:, h : h + 1] * incoming[:, cols]
            state = local[rows, cols] + fade[:, h : h + 1] * base
            dechunked[rows, cols] = state.astype(BF16)
            earlier = jnp.where(top, base, pltpu.roll(state, 1, 0))
            full = adjoint[rows, cols] + fade_back[:, h : h + 1] * tail[:, cols]
            total = total + (decay[:, h : h + 1] * full) * (values[rows, cols] - earlier)
        stats = stats_ref[rows, :]
        iq, ik, cosine, active = (stats[:, i : i + 1] for i in range(4))
        d_cos = -0.5 * (active * jnp.sum(total, -1, keepdims=True))
        both = d_cos * (iq * ik)
        over_q, over_k = d_cos * (cosine * iq * iq), d_cos * (cosine * ik * ik)
        q, k = queries[rows, :], keys[rows, :]
        d_query[rows, :] = (k * both - over_q * q).astype(BF16)
        d_prev[rows, :] = (q * both - over_k * k).astype(BF16)
        block_copy(dechunked, dechunked_out, d_sems, n).start()
        return before + last

    lax.fori_loop(0, blocks, block, jnp.zeros((1, LANES), F32))
    for n in range(blocks):
        block_copy(dechunked, dechunked_out, d_sems, n).wait()


def share_kernel(place, turned, d, share):
    step = 512
    rows = share.shape[0] // 2
    for i in range(d.shape[1] // step):
        part = slice(i * step, (i + 1) * step)
        for b in range(2):
            share[b * rows : (b + 1) * rows, part] = mxu(
                side_rows(1 - place[0] % 2, turned, b), d[:, part]
            ).astype(BF16)


def up_sum_kernel(place, d_values, theirs, turned, out):
    add_share(place, turned, d_values, theirs, out, out.shape[1] - d_values.shape[1])


def route_sum_kernel(place, d, theirs, partial, turned, out, *, at):
    add_share(place, turned, d, theirs, out, at)


def add_share(place, turned, d, theirs, out, at):
    step = 512
    rows = theirs.shape[0] // 2
    for i in range(d.shape[1] // step):
        part = slice(i * step, (i + 1) * step)
        for b in range(2):
            half = slice(b * rows, (b + 1) * rows)
            mine = mxu(side_rows(place[0] % 2, turned, b), d[:, part])
            total = mine + theirs[half, part].astype(F32)
            out[half, at + i * step : at + (i + 1) * step] = total.astype(BF16)


def tokens_kernel(place, d_query_in, d_key_in, d_values_in, *refs):
    pieces, out = refs[:16], refs[16]
    d_query, d_key, d_values, wq, wk, wu, d_sems, q_sems, k_sems, u_sems = refs[17:]
    loads = [
        whole_copy(source, target, d_sems.at[i])
        for i, (source, target) in enumerate(
            ((d_query_in, d_query), (d_key_in, d_key), (d_values_in, d_values))
        )
    ]
    for side in range(2):
        two, four = slice(2 * side, 2 * side + 2), slice(4 * side, 4 * side + 4)
        loads += fetch_panel(place, pieces[:4][two], wq.at[side], q_sems.at[side])
        loads += fetch_panel(place, pieces[4:8][two], wk.at[side], k_sems.at[side])
        loads += fetch_panel(place, pieces[8:][four], wu.at[side], u_sems.at[side])
    for c in loads:
        c.start()
    for c in loads:
        c.wait()
    dims = (((1,), (1,)), ((), ()))
    for side in range(2):
        index = side + (1 - 2 * side) * (place[0] // 2)
        terms = [
            lax.dot_general(d[...], w[side], dims, preferred_element_type=F32)
            for d, w in ((d_query, wq), (d_key, wk), (d_values, wu))
        ]
        out[:, panel_columns(index, wq.shape[1])] = (terms[0] + terms[1] + terms[2]).astype(BF16)


def sum_kernel(parts, out):
    step = 512
    for i in range(out.shape[2] // step):
        cols = slice(i * step, (i + 1) * step)
        acc = parts[0, :, cols].astype(F32)
        for j in range(1, parts.shape[0]):
            acc = acc + parts[j, :, cols].astype(F32)
        rounded = acc.astype(BF16)
        for j in range(out.shape[0]):
            out[j, :, cols] = rounded


def sum_ranks(exchanged, copies):
    _, depth, width = exchanged.shape
    return pl.pallas_call(
        sum_kernel,
        out_shape=jax.ShapeDtypeStruct((copies, depth, width), BF16),
        in_specs=[VMEM],
        out_specs=VMEM,
        compiler_params=pltpu.CompilerParams(vmem_limit_bytes=16 << 20),
    )(exchanged)


def widen_kernel(parts, *refs):
    outs, bufs, sems = refs[:3], refs[3:6], refs[6]
    ranks, depth, _ = parts.shape
    chunks = 4
    group = ranks // chunks
    copies = []
    for i in range(chunks):
        start = 0
        for o, (out, buf) in enumerate(zip(outs, bufs)):
            width = out.shape[1]
            for j in range(i * group, (i + 1) * group):
                buf[j * depth : (j + 1) * depth, :] = parts[j, :, start : start + width].astype(F32)
            rows = pl.ds(i * group * depth, group * depth)
            copies.append(
                pltpu.make_async_copy(buf.at[rows, :], out.at[rows, :], sems.at[o * chunks + i])
            )
            copies[-1].start()
            start += width
    for c in copies:
        c.wait()


def widen(summed, widths):
    ranks, depth, _ = summed.shape
    shapes = [(ranks * depth, w) for w in widths]
    return pl.pallas_call(
        widen_kernel,
        out_shape=[jax.ShapeDtypeStruct(s, F32) for s in shapes],
        in_specs=[VMEM],
        out_specs=[HBM] * len(widths),
        scratch_shapes=[pltpu.VMEM(s, F32) for s in shapes] + [DMA((12,))],
        compiler_params=pltpu.CompilerParams(vmem_limit_bytes=16 << 20),
    )(summed)


SMEM = pl.BlockSpec(memory_space=pltpu.SMEM)
VMEM = pl.BlockSpec(memory_space=pltpu.VMEM)
HBM = pl.BlockSpec(memory_space=pltpu.HBM)
DMA = pltpu.SemaphoreType.DMA


def in_hbm(a):
    return pltpu.with_memory_space_constraint(a, pltpu.HBM)


def call(
    body, place, vmem_args, hbm_args, vmem_outs, hbm_outs, scratch, flops, limit, aliases=None
):
    return pl.pallas_call(
        body,
        out_shape=[jax.ShapeDtypeStruct(s, t) for s, t in vmem_outs]
        + [pltpu.HBM(s, t) for s, t in hbm_outs],
        in_specs=[SMEM] + [VMEM] * len(vmem_args) + [HBM] * len(hbm_args),
        out_specs=[VMEM] * len(vmem_outs) + [HBM] * len(hbm_outs),
        scratch_shapes=scratch,
        input_output_aliases=aliases or {},
        cost_estimate=pl.CostEstimate(flops=flops, bytes_accessed=1 << 20, transcendentals=0),
        compiler_params=pltpu.CompilerParams(vmem_limit_bytes=limit << 20),
    )(place, *vmem_args, *[in_hbm(a) for a in hbm_args])


def local_step(tokens, bounds, decay_rates, w_query, w_key, w_up, grad_out):
    _, length, width = tokens.shape
    hidden = w_up.shape[1]
    heads = decay_rates.shape[0]
    rows = w_query.shape[0]
    blocks = length // SPAN
    tok, cot = tokens[0], grad_out[0]
    core, high = lax.axis_index("core"), lax.axis_index("xh")
    place = jnp.stack(
        [lax.axis_index("xl") * 2 + core, lax.axis_index("z"), high]
    ).astype(jnp.int32)

    half = rows // 2
    up = (w_up[:half], w_up[half:])
    q2, k2 = along_x(w_query, -1), along_x(w_key, 1)
    q1, k1 = swap_core(w_query), swap_core(w_key)
    before = along_ctx(tok[-1:], 1)
    u2_low = along_x(up[0], -1)
    u2_high = along_x(up[1], 1)
    tok_prev = jnp.concatenate([before, tok[:-1]], 0)

    decay = jnp.pad(decay_rates, (0, LANES - heads))[None]
    ready, decay, place = lax.optimization_barrier((tok, decay, place))
    flat, wide, narrow = (length, width), (length, hidden), (length, LANES)
    square, tall, per_block = (2 * rows, width), (2 * rows, hidden), (blocks, hidden)
    buf = pltpu.VMEM
    q_part, turned = call(
        near_kernel, place, (ready,), (w_query, q1),
        ((flat, F32), ((width, length), BF16)), (),
        [buf(square, BF16), DMA((2,))], 1_000_000_000, 12,
    )
    q_part, up_low, up_high, q2, k2 = lax.optimization_barrier((q_part, *up, q2, k2))
    q3, k3 = swap_core(q2), swap_core(k2)
    u1 = (swap_core(up_low), swap_core(up_high))
    v_part, turned_prev = call(
        near_values_kernel, place, (tok, tok_prev), (*up, *u1),
        ((wide, F32), ((width, length), BF16)), (),
        [buf(tall, BF16), DMA((4,))], 2_000_000_000, 12,
    )
    queries, keys, local_adjoint, mix, keep, stats, outs, b_carry = call(
        rates_kernel, place,
        (bounds, decay, tok, tok_prev, cot, q_part),
        (q2, q3, w_key, k1, k2, k3),
        ((flat, F32), (flat, F32), (wide, F32), (narrow, F32), (narrow, F32), (narrow, F32),
         (per_block, F32), ((2, hidden), F32)),
        (),
        [buf(square, BF16), buf((width, width), BF16), DMA((2,)), DMA((2, 2))],
        6_000_000_000, 16,
    )
    u2_low, u2_high, keep_late = lax.optimization_barrier((u2_low, u2_high, keep))
    u3 = (swap_core(u2_low), swap_core(u2_high))
    values, local_states, ins, message = call(
        states_kernel, place,
        (mix, keep_late, tok, b_carry, v_part),
        (u2_low, u2_high, *u3),
        ((wide, F32), (wide, F32), (per_block, F32), ((3, hidden), F32)),
        (),
        [buf(tall, BF16), buf((1, hidden), F32), DMA((4,))],
        6_000_000_000, 16,
    )
    other = lax.ppermute(message, "xh", [(0, 1), (1, 0)])
    (pair,) = call(
        pair_kernel, place, (message, other), (), (((3, hidden), F32),), (), [], 1_000_000, 4
    )
    messages = [other] + [
        lax.ppermute(pair, "z", [(i, (i - d) % 4) for i in range(4)]) for d in (1, 2, 3)
    ]

    half_flat, half_wide = (2 * rows, width), (2 * rows, hidden)
    d_values, tails, up_share = call(
        adjoint_kernel, place,
        (outs, mix, keep, *messages, local_adjoint, turned),
        (),
        ((wide, BF16), (per_block, F32)),
        ((half_wide, BF16),),
        [buf(half_wide, BF16), DMA((4,))],
        3_000_000_000, 16,
    )
    up_theirs = swap_core(up_share)
    d_query, d_prev, dechunked = call(
        router_kernel, place,
        (ins, tails, keep, stats, decay, *messages, local_states, values, local_adjoint,
         queries, keys),
        (),
        ((flat, BF16), (flat, BF16)),
        ((wide, BF16),),
        [buf(wide, BF16), DMA((blocks,))],
        3_000_000_000, 16,
    )
    after = along_ctx(d_prev[:1], -1)
    (q_share,) = call(
        share_kernel, place, (turned, d_query), (), ((half_flat, BF16),), (), [], 500_000_000, 6
    )
    q_theirs = swap_core(q_share)
    d_prev_late, q_share = lax.optimization_barrier((d_prev, q_share))
    (k_share,) = call(
        share_kernel, place, (turned_prev, d_prev_late), (), ((half_flat, BF16),), (), [],
        500_000_000, 6,
    )
    k_theirs = swap_core(k_share)
    full = (2 * rows, 2 * width + hidden)
    (partial,) = call(
        up_sum_kernel, place,
        (d_values, up_theirs, turned), (), ((full, BF16),), (), [], 1_500_000_000, 8,
    )
    sums = partial
    for d, theirs, lhs, at in (
        (d_query, q_theirs, turned, 0), (d_prev, k_theirs, turned_prev, width)
    ):
        (sums,) = call(
            functools.partial(route_sum_kernel, at=at), place,
            (d, theirs, sums, lhs), (), ((full, BF16),), (), [], 700_000_000, 8, {3: 0},
        )
    pair_sum = sums
    exchanged = lax.all_to_all(
        pair_sum.reshape(64, -1, pair_sum.shape[1]), ("xl", "dp", "z", "xh"), 0, 0, tiled=True
    )
    summed = lax.all_to_all(sum_ranks(exchanged, 32), ("dp", "z", "xh"), 0, 0, tiled=True)

    d_key = jnp.concatenate([d_prev[1:], after], 0)
    (grad_tokens,) = call(
        tokens_kernel, place,
        (),
        (d_query, d_key, d_values, w_query, q1, q2, q3, w_key, k1, k2, k3,
         *up, *u1, u2_low, u2_high, *u3),
        ((flat, BF16),),
        (),
        [buf(flat, BF16), buf(flat, BF16), buf(wide, BF16), buf((2, *square), BF16),
         buf((2, *square), BF16), buf((2, *tall), BF16), DMA((3,)), DMA((2, 2)), DMA((2, 2)),
         DMA((2, 4))],
        5_000_000_000, 60,
    )
    grads = widen(summed, (width, width, hidden))
    return (dechunked[None], grad_tokens[None], *grads)


def solution(mesh):
    split = jax.sharding.Mesh(
        mesh.devices.reshape(4, 2, 2, 4, 2), ("dp", "xl", "core", "z", "xh")
    )
    rows = P(("xl", "core"), None)
    data = P(("dp", "xl", "core"), CTX, None)
    return jax.shard_map(
        local_step,
        mesh=split,
        in_specs=(data, P(("dp", "xl", "core"), CTX), P(), rows, rows, rows, data),
        out_specs=(data, data, rows, rows, rows),
        check_vma=False,
    )
```

profile of v0, /device:TPU:0, one launch (start us, length us, event | category | flops | bytes accessed | tf_op | source)
XLA Modules:
  0.0 200.2 jit_solution(1067312447345817113)
XLA Ops:
  0.7 0.1 collective-permute-start.1
  0.7 2.9 %collective-permute-start.2 = (bf16[256,1024]{1,0:T(8,128)(2,1)}, bf16[256,1024]{1,0:T(8,128)(2,1)}, u32[]{:S(2)}, u32[]{:S(2)}) collective-permute-start(bf16[256,1024]{1,0:T(8,128)(2,1)} %refs_0_.1), channel_id=1, source_target_pairs={{0,17},{1,16},{16,0},{17,1},{2,19},{3,18},{18,2},{19,3},{4,21},{5,... | collective-permute-start | bytes 1572872 | tf_op jit(solution)/shard_map/ppermute | solution.py:27
  3.7 0.1 collective-permute-start.5
  3.8 0.0 collective-permute-start.3
  3.8 2.3 %fusion = (bf16[128,2048]{1,0:T(8,128)(2,1)}, bf16[128,2048]{1,0:T(8,128)(2,1)}) fusion(bf16[256,2048]{1,0:T(8,128)(2,1)} %param.12), kind=kLoop, calls=%fused_computation.6 | loop fusion | bytes 2097152 | tf_op jit(solution)/shard_map/slice | solution.py:495
  6.1 0.8 collective-permute-start.8
  6.9 0.1 pad_add_fusion.place
  7.0 0.0 collective-permute-done.1.q1.refs_1_
  7.0 0.8 copy-done.7
  7.8 2.5 %shard_map.110 = (f32[512,1024]{1,0:T(8,128)S(1)}, bf16[1024,512]{1,0:T(8,128)(2,1)S(1)}) custom-call(s32[3]{0:T(128)S(1)} %pad_add_fusion.place, bf16[512,1024]{1,0:T(8,128)(2,1)S(1)} %bitcast.15, bf16[256,1024]{1,0:T(8,128)(2,1)} %refs_0_.1, bf16[256,1024]{1,0:T(8,128)(2,1)} %copy-done.7), custom_call_target="tpu_custom_call" | custom-call | flops 1000000000 | bytes 1048576 | tf_op jit(solution)/shard_map/pallas_call | solution.py:469
  10.3 5.5 %collective-permute-done.2.q2.refs_2_ = bf16[256,1024]{1,0:T(8,128)(2,1)} collective-permute-done((bf16[256,1024]{1,0:T(8,128)(2,1)}, bf16[256,1024]{1,0:T(8,128)(2,1)}, u32[]{:S(2)}, u32[]{:S(2)}) %collective-permute-start.2) | collective-permute-done | bytes 524320 | tf_op jit(solution)/shard_map/ppermute | solution.py:27
  15.8 4.4 %collective-permute-done.3.k2.refs_6_ = bf16[256,1024]{1,0:T(8,128)(2,1)} collective-permute-done((bf16[256,1024]{1,0:T(8,128)(2,1)}, bf16[256,1024]{1,0:T(8,128)(2,1)}, u32[]{:S(2)}, u32[]{:S(2)}) %collective-permute-start.3) | collective-permute-done | bytes 524320 | tf_op jit(solution)/shard_map/ppermute | solution.py:27
  20.2 0.5 collective-permute-start.6
  20.7 0.0 copy-start.4
  20.7 0.0 copy-start.5
  20.7 1.6 collective-permute-start
  22.3 0.1 slice_bitcast_fusion
  22.4 5.0 %collective-permute-done = bf16[1,1024]{1,0:T(2,128)(2,1)S(1)} collective-permute-done((bf16[1,1024]{1,0:T(2,128)(2,1)S(1)}, bf16[1,1024]{1,0:T(2,128)(2,1)S(1)}, u32[]{:S(2)}, u32[]{:S(2)}) %collective-permute-start) | collective-permute-done | bytes 2080 | tf_op jit(solution)/shard_map/ppermute | solution.py:35
  27.4 0.0 collective-permute-start.7
  27.5 0.3 pad_maximum_fusion.tok_prev
  27.7 0.0 collective-permute-done.5.k1.refs_5_
  27.8 0.1 collective-permute-start.9
  27.8 0.0 collective-permute-done.4.q3.refs_3_
  27.9 0.5 collective-permute-start.10
  28.4 0.0 collective-permute-done.6.k3.refs_7_
  28.4 0.3 copy-done.8
  28.6 0.5 copy-done.9
  29.2 9.0 %shard_map.111 = (f32[512,1024]{1,0:T(8,128)S(1)}, f32[512,1024]{1,0:T(8,128)S(1)}, f32[512,2048]{1,0:T(8,128)S(1)}, f32[512,128]{1,0:T(8,128)S(1)}, f32[512,128...) custom-call(s32[3]{0:T(128)S(1)} %pad_add_fusion.place, ...), custom_call_target="tpu_custom_call" | custom-call | flops 6000000000 | bytes 1048576 | tf_op jit(solution)/shard_map/pallas_call | solution.py:469
  38.2 2.8 %collective-permute-done.7.u4.refs_12_ = bf16[128,2048]{1,0:T(8,128)(2,1)S(1)} collective-permute-done((bf16[128,2048]{1,0:T(8,128)(2,1)S(1)}, bf16[128,2048]{1,0:T(8,128)(2,1)S(1)}, u32[]{:S(2)}, u32[]{:S(2)}) %collective-permute-start.7) | collective-permute-done | bytes 524320 | tf_op jit(solution)/shard_map/ppermute | solution.py:27
  41.0 0.5 collective-permute-start.12
  41.5 0.8 copy-done.11
  42.3 0.8 copy-done.12
  43.1 3.4 %shard_map.112 = (f32[512,2048]{1,0:T(8,128)S(1)}, bf16[1024,512]{1,0:T(8,128)(2,1)S(1)}) custom-call(s32[3]{0:T(128)S(1)} %pad_add_fusion.place, bf16[512,1024]{1,0:T(8,128)(2,1)S(1)} %bitcast.17, bf16[512,1024]{1,0:T(8,128)(2,1)S(1)} %pad_maximum_fusion.tok_prev, bf16[128,2048]{1,0:T(8,128)(2,1)} %get-tuple-element.53.u0.refs_8_, ...), custom_call_target="tpu_custom_call" | custom-call | flops 2000000000 | bytes 1048576 | tf_op jit(solution)/shard_map/pallas_call | solution.py:469
  46.5 0.8 copy-done.13
  47.3 0.1 copy-done.14
  47.5 7.0 %shard_map.113 = (f32[512,2048]{1,0:T(8,128)S(1)}, f32[512,2048]{1,0:T(8,128)S(1)}, f32[4,2048]{1,0:T(4,128)S(1)}, f32[3,2048]{1,0:T(4,128)S(1)}) custom-call(s32[3]{0:T(128)S(1)} %pad_add_fusion.place, f32[512,128]{1,0:T(8,128)S(1)} %get-tuple-element.49.mix_ref, f32[512,128]{1,0:T(8,128)S(1)} %get-tuple-element.51.keep_ref, ...), custom_call_target="tpu_custom_call" | custom-call | flops 6000000000 | bytes 1048576 | tf_op jit(solution)/shard_map/pallas_call | solution.py:469
  54.5 3.8 %collective-permute-start.13 = (f32[3,2048]{1,0:T(4,128)S(1)}, f32[3,2048]{1,0:T(4,128)S(1)}, u32[]{:S(2)}, u32[]{:S(2)}) collective-permute-start(f32[3,2048]{1,0:T(4,128)S(1)} %get-tuple-element.60.message), channel_id=1, source_target_pairs={{0,1},{1,0},{2,3},{3,2},{4,5},{5,4},{6,7},{7,6},{8,9},{9,8},{10,11... | collective-permute-start | bytes 73736 | tf_op jit(solution)/shard_map/ppermute | solution.py:542
  58.3 1.9 collective-permute-done.13.other
  60.2 0.6 shard_map.114
  60.7 3.3 %collective-permute-start.16 = (f32[3,2048]{1,0:T(4,128)S(1)}, f32[3,2048]{1,0:T(4,128)S(1)}, u32[]{:S(2)}, u32[]{:S(2)}) collective-permute-start(f32[3,2048]{1,0:T(4,128)S(1)} %shard_map.114), channel_id=1, source_target_pairs={{0,2},{2,4},{4,6},{6,0},{1,3},{3,5},{5,7},{7,1},{8,10},{10,12},{12... | collective-permute-start | bytes 73736 | tf_op jit(solution)/shard_map/ppermute | solution.py:547
  64.0 3.9 %collective-permute-start.15 = (f32[3,2048]{1,0:T(4,128)S(1)}, f32[3,2048]{1,0:T(4,128)S(1)}, u32[]{:S(2)}, u32[]{:S(2)}) collective-permute-start(f32[3,2048]{1,0:T(4,128)S(1)} %shard_map.114), channel_id=1, source_target_pairs={{0,4},{2,6},{4,0},{6,2},{1,5},{3,7},{5,1},{7,3},{8,12},{10,14},{12... | collective-permute-start | bytes 73736 | tf_op jit(solution)/shard_map/ppermute | solution.py:547
  67.9 0.7 collective-permute-start.14
  68.6 1.5 collective-permute-done.15.next2
  70.1 1.7 collective-permute-done.14.next1
  71.8 5.3 %shard_map.115 = (bf16[512,2048]{1,0:T(8,128)(2,1)S(1)}, f32[4,2048]{1,0:T(4,128)S(1)}, bf16[512,2048]{1,0:T(8,128)(2,1)}) custom-call(s32[3]{0:T(128)S(1)} %pad_add_fusion.place, f32[4,2048]{1,0:T(4,128)S(1)} %get-tuple-element.59.outs, f32[512,128]{1,0:T(8,128)S(1)} %get-tuple-element.49.mix_ref, f32[512,128]{1,0:T(8,128)S(1)} %get-tuple-element.51.keep_ref, ...), custom_call_target="tpu_custom_call" | custom-call | flops 3000000000 | bytes 1048576 | tf_op jit(solution)/shard_map/pallas_call | solution.py:469
  77.1 0.1 collective-permute-start.20
  77.2 6.8 %shard_map.116 = (bf16[512,1024]{1,0:T(8,128)(2,1)S(1)}, bf16[512,1024]{1,0:T(8,128)(2,1)S(1)}, bf16[512,2048]{1,0:T(8,128)(2,1)}) custom-call(s32[3]{0:T(128)S(1)} %pad_add_fusion.place, f32[4,2048]{1,0:T(4,128)S(1)} %get-tuple-element.58.ins, f32[4,2048]{1,0:T(4,128)S(1)} %get-tuple-element.63.tails, f32[512,128]{1,0:T(8,128)S(1)} %get-tuple-element.51.keep_ref, ...), custom_call_target="tpu_custom_call" | custom-call | flops 3000000000 | bytes 1048576 | tf_op jit(solution)/shard_map/pallas_call | solution.py:469
  84.0 0.0 copy-start
  84.0 1.2 shard_map.118
  85.2 0.6 collective-permute-start.19
  85.8 1.2 shard_map.119
  87.1 0.1 collective-permute-start.18
  87.2 1.9 shard_map.120.partial
  89.1 1.3 shard_map.121.partial
  90.4 1.3 shard_map.122
  91.6 61.0 %all_to_all.10.parts = bf16[64,8,4096]{2,1,0:T(8,128)(2,1)S(1)} all-to-all(bf16[64,8,4096]{2,1,0:T(8,128)(2,1)S(1)} %bitcast.14), channel_id=1, replica_groups=mesh['dp'=4,'xl'=2,'core'=2,'z'=4,'xh'=2] {'xl','dp','z','xh'}, dimensions={0} | all-to-all | bytes 8388608 | tf_op jit(solution)/shard_map/all_to_all | solution.py:596
  152.6 2.0 %shard_map.123 = bf16[32,8,4096]{2,1,0:T(8,128)(2,1)} custom-call(bf16[64,8,4096]{2,1,0:T(8,128)(2,1)S(1)} %all_to_all.10.parts), custom_call_target="tpu_custom_call" | custom-call | tf_op jit(solution)/shard_map/pallas_call | solution.py:412
  154.6 5.0 %all-to-all-start.1 = ((bf16[32,8,4096]{2,1,0:T(8,128)(2,1)}), bf16[32,8,4096]{2,1,0:T(8,128)(2,1)S(1)}, u32[]{:S(2)}, u32[]{:S(2)}) async-start(bf16[32,8,4096]{2,1,0:T(8,128)(2,1)} %shard_map.123), calls=%async_computation.1 | async-start | bytes 4194304 | tf_op jit(solution)/shard_map/all_to_all | solution.py:599
  159.6 1.5 collective-permute-start.17
  161.2 0.3 slice.30
  161.4 24.5 %collective-permute-done.17 = bf16[1,1024]{1,0:T(2,128)(2,1)S(1)} collective-permute-done((bf16[1,1024]{1,0:T(2,128)(2,1)S(1)}, bf16[1,1024]{1,0:T(2,128)(2,1)S(1)}, u32[]{:S(2)}, u32[]{:S(2)}) %collective-permute-start.17) | collective-permute-done | bytes 2080 | tf_op jit(solution)/shard_map/ppermute | solution.py:35
  185.9 1.1 pad_maximum_fusion.1.d_key_in
  187.0 10.9 %shard_map.117 = bf16[512,1024]{1,0:T(8,128)(2,1)} custom-call(s32[3]{0:T(128)} %copy-done.3, bf16[512,1024]{1,0:T(8,128)(2,1)} %copy-done, bf16[512,1024]{1,0:T(8,128)(2,1)} %pad_maximum_fusion.1.d_key_in, bf16[512,2048]{1,0:T(8,128)(2,1)} %copy-done.1, bf16[256,1024]{1,0:T(8,128)(2,1)} %refs_0_.1, bf16[256,1024]{1,0:T(8,128)(2,1)} %copy-done.7, ...), custom_call_target="tpu_custom_call" | custom-call | flops 5000000000 | bytes 1048576 | tf_op jit(solution)/shard_map/pallas_call | solution.py:469
  197.9 2.1 %shard_map.124 = (f32[256,1024]{1,0:T(8,128)}, f32[256,1024]{1,0:T(8,128)}, f32[256,2048]{1,0:T(8,128)}) custom-call(bf16[32,8,4096]{2,1,0:T(8,128)(2,1)S(1)} %all-to-all-done.1.parts), custom_call_target="tpu_custom_call" | custom-call | tf_op jit(solution)/shard_map/pallas_call | solution.py:446
  (37 shorter events, 0.1 us)
Async XLA Ops:
  0.6 6.3 %copy-start.15 = (f32[16]{0:T(128)S(1)}, f32[16]{0:T(128)}, u32[]{:S(2)}) copy-start(f32[16]{0:T(128)} %param.9) | copy-start | bytes 196
  0.6 7.1 %copy-start.2 = (bf16[1,512,1024]{2,1,0:T(8,128)(2,1)S(1)}, bf16[1,512,1024]{2,1,0:T(8,128)(2,1)}, u32[]{:S(2)}) copy-start(bf16[1,512,1024]{2,1,0:T(8,128)(2,1)} %param.7) | copy-start | bytes 3145732
  0.7 6.3 %collective-permute-start.1 = (bf16[256,1024]{1,0:T(8,128)(2,1)}, bf16[256,1024]{1,0:T(8,128)(2,1)S(1)}, u32[]{:S(2)}, u32[]{:S(2)}) collective-permute-start(bf16[256,1024]{1,0:T(8,128)(2,1)} %refs_0_.1), channel_id=1, source_target_pairs={{0,8},{8,0},{1,9},{9,1},{2,10},{10,2},{3,11},{11,3},{4,12},{12,4},... | collective-permute-start | bytes 1572872 | tf_op jit(solution)/shard_map/ppermute | solution.py:31
  0.7 15.0 %collective-permute-start.2 = (bf16[256,1024]{1,0:T(8,128)(2,1)}, bf16[256,1024]{1,0:T(8,128)(2,1)}, u32[]{:S(2)}, u32[]{:S(2)}) collective-permute-start(bf16[256,1024]{1,0:T(8,128)(2,1)} %refs_0_.1), channel_id=1, source_target_pairs={{0,17},{1,16},{16,0},{17,1},{2,19},{3,18},{18,2},{19,3},{4,21},{5,... | collective-permute-start | bytes 1572872 | tf_op jit(solution)/shard_map/ppermute | solution.py:27
  3.7 24.1 %collective-permute-start.5 = (bf16[256,1024]{1,0:T(8,128)(2,1)}, bf16[256,1024]{1,0:T(8,128)(2,1)}, u32[]{:S(2)}, u32[]{:S(2)}) collective-permute-start(bf16[256,1024]{1,0:T(8,128)(2,1)} %refs_4_.1), channel_id=1, source_target_pairs={{0,8},{8,0},{1,9},{9,1},{2,10},{10,2},{3,11},{11,3},{4,12},{12,4},... | collective-permute-start | bytes 1572872 | tf_op jit(solution)/shard_map/ppermute | solution.py:31
  3.8 16.3 %collective-permute-start.3 = (bf16[256,1024]{1,0:T(8,128)(2,1)}, bf16[256,1024]{1,0:T(8,128)(2,1)}, u32[]{:S(2)}, u32[]{:S(2)}) collective-permute-start(bf16[256,1024]{1,0:T(8,128)(2,1)} %refs_4_.1), channel_id=1, source_target_pairs={{0,16},{1,17},{16,1},{17,0},{2,18},{3,19},{18,3},{19,2},{4,20},{5,... | collective-permute-start | bytes 1572872 | tf_op jit(solution)/shard_map/ppermute | solution.py:27
  6.1 32.1 %collective-permute-start.8 = (bf16[128,2048]{1,0:T(8,128)(2,1)}, bf16[128,2048]{1,0:T(8,128)(2,1)}, u32[]{:S(2)}, u32[]{:S(2)}) collective-permute-start(bf16[128,2048]{1,0:T(8,128)(2,1)} %get-tuple-element.54.u1.refs_9_), channel_id=1, source_target_pairs={{0,16},{1,17},{16,1},{17,0},{2,18},{3,19},{18,3},{19,2},{4,20},{5,... | collective-permute-start | bytes 1572872 | tf_op jit(solution)/shard_map/ppermute | solution.py:27
  7.0 83.4 %copy-start.3 = (s32[3]{0:T(128)}, s32[3]{0:T(128)S(1)}, u32[]{:S(2)}) copy-start(s32[3]{0:T(128)S(1)} %pad_add_fusion.place) | copy-start | bytes 40
  7.0 20.5 %copy-start.6 = (bf16[128,2048]{1,0:T(8,128)(2,1)S(1)}, bf16[128,2048]{1,0:T(8,128)(2,1)}, u32[]{:S(2)}) copy-start(bf16[128,2048]{1,0:T(8,128)(2,1)} %get-tuple-element.53.u0.refs_8_) | copy-start | bytes 1572868
  7.0 0.8 copy-start.7
  20.2 7.7 %collective-permute-start.4 = (bf16[256,1024]{1,0:T(8,128)(2,1)}, bf16[256,1024]{1,0:T(8,128)(2,1)S(1)}, u32[]{:S(2)}, u32[]{:S(2)}) collective-permute-start(bf16[256,1024]{1,0:T(8,128)(2,1)} %collective-permute-done.2.q2.refs_2_), channel_id=1, source_target_pairs={{0,8},{8,0},{1,9},{9,1},{2,10},{10,2},{3,11},{11,3},{4,12},{12,4},... | collective-permute-start | bytes 1572872 | tf_op jit(solution)/shard_map/ppermute | solution.py:31
  20.2 8.2 %collective-permute-start.6 = (bf16[256,1024]{1,0:T(8,128)(2,1)}, bf16[256,1024]{1,0:T(8,128)(2,1)S(1)}, u32[]{:S(2)}, u32[]{:S(2)}) collective-permute-start(bf16[256,1024]{1,0:T(8,128)(2,1)} %collective-permute-done.3.k2.refs_6_), channel_id=1, source_target_pairs={{0,8},{8,0},{1,9},{9,1},{2,10},{10,2},{3,11},{11,3},{4,12},{12,4},... | collective-permute-start | bytes 1572872 | tf_op jit(solution)/shard_map/ppermute | solution.py:31
  20.7 8.5 %copy-start.4 = (bf16[1,512,2048]{2,1,0:T(8,128)(2,1)S(1)}, bf16[1,512,2048]{2,1,0:T(8,128)(2,1)}, u32[]{:S(2)}) copy-start(bf16[1,512,2048]{2,1,0:T(8,128)(2,1)} %param.13) | copy-start | bytes 6291460
  20.7 8.5 %copy-start.5 = (s32[1,512]{1,0:T(1,128)S(1)}, s32[1,512]{1,0:T(1,128)}, u32[]{:S(2)}) copy-start(s32[1,512]{1,0:T(1,128)} %bounds.1) | copy-start | bytes 6148
  20.7 6.7 %collective-permute-start = (bf16[1,1024]{1,0:T(2,128)(2,1)S(1)}, bf16[1,1024]{1,0:T(2,128)(2,1)S(1)}, u32[]{:S(2)}, u32[]{:S(2)}) collective-permute-start(bf16[1,1024]{1,0:T(2,128)(2,1)S(1)} %slice_bitcast_fusion.1), channel_id=1, source_target_pairs={{0,1},{1,2},{2,3},{3,4},{4,5},{5,6},{6,7},{8,9},{9,10},{10,11},{11... | collective-permute-start | bytes 6152 | tf_op jit(solution)/shard_map/ppermute | solution.py:35
  27.4 13.6 %collective-permute-start.7 = (bf16[128,2048]{1,0:T(8,128)(2,1)S(1)}, bf16[128,2048]{1,0:T(8,128)(2,1)S(1)}, u32[]{:S(2)}, u32[]{:S(2)}) collective-permute-start(bf16[128,2048]{1,0:T(8,128)(2,1)S(1)} %copy-done.6), channel_id=1, source_target_pairs={{0,17},{1,16},{16,0},{17,1},{2,19},{3,18},{18,2},{19,3},{4,21},{5,... | collective-permute-start | bytes 1572872 | tf_op jit(solution)/shard_map/ppermute | solution.py:27
  27.8 13.8 %collective-permute-start.9 = (bf16[128,2048]{1,0:T(8,128)(2,1)S(1)}, bf16[128,2048]{1,0:T(8,128)(2,1)S(1)}, u32[]{:S(2)}, u32[]{:S(2)}) collective-permute-start(bf16[128,2048]{1,0:T(8,128)(2,1)S(1)} %copy-done.6), channel_id=1, source_target_pairs={{0,8},{8,0},{1,9},{9,1},{2,10},{10,2},{3,11},{11,3},{4,12},{12,4},... | collective-permute-start | bytes 1572872 | tf_op jit(solution)/shard_map/ppermute | solution.py:31
  27.9 0.8 copy-start.8
  27.9 13.7 %collective-permute-start.10 = (bf16[128,2048]{1,0:T(8,128)(2,1)}, bf16[128,2048]{1,0:T(8,128)(2,1)S(1)}, u32[]{:S(2)}, u32[]{:S(2)}) collective-permute-start(bf16[128,2048]{1,0:T(8,128)(2,1)} %get-tuple-element.54.u1.refs_9_), channel_id=1, source_target_pairs={{0,8},{8,0},{1,9},{9,1},{2,10},{10,2},{3,11},{11,3},{4,12},{12,4},... | collective-permute-start | bytes 1572872 | tf_op jit(solution)/shard_map/ppermute | solution.py:31
  28.4 0.8 copy-start.9
  41.0 5.5 %copy-start.10 = (bf16[128,2048]{1,0:T(8,128)(2,1)}, bf16[128,2048]{1,0:T(8,128)(2,1)S(1)}, u32[]{:S(2)}) copy-start(bf16[128,2048]{1,0:T(8,128)(2,1)S(1)} %collective-permute-done.7.u4.refs_12_) | copy-start | bytes 1572868
  41.0 5.5 %collective-permute-start.11 = (bf16[128,2048]{1,0:T(8,128)(2,1)S(1)}, bf16[128,2048]{1,0:T(8,128)(2,1)S(1)}, u32[]{:S(2)}, u32[]{:S(2)}) collective-permute-start(bf16[128,2048]{1,0:T(8,128)(2,1)S(1)} %collective-permute-done.7.u4.refs_12_), channel_id=1, source_target_pairs={{0,8},{8,0},{1,9},{9,1},{2,10},{10,2},{3,11},{11,3},{4,12},{12,4},... | collective-permute-start | bytes 1572872 | tf_op jit(solution)/shard_map/ppermute | solution.py:31
  41.0 5.5 %collective-permute-start.12 = (bf16[128,2048]{1,0:T(8,128)(2,1)}, bf16[128,2048]{1,0:T(8,128)(2,1)S(1)}, u32[]{:S(2)}, u32[]{:S(2)}) collective-permute-start(bf16[128,2048]{1,0:T(8,128)(2,1)} %collective-permute-done.8.u5.refs_13_), channel_id=1, source_target_pairs={{0,8},{8,0},{1,9},{9,1},{2,10},{10,2},{3,11},{11,3},{4,12},{12,4},... | collective-permute-start | bytes 1572872 | tf_op jit(solution)/shard_map/ppermute | solution.py:31
  41.5 0.8 copy-start.11
  42.3 0.8 copy-start.12
  46.5 0.8 copy-start.13
  46.5 1.0 copy-start.14
  54.5 5.6 %collective-permute-start.13 = (f32[3,2048]{1,0:T(4,128)S(1)}, f32[3,2048]{1,0:T(4,128)S(1)}, u32[]{:S(2)}, u32[]{:S(2)}) collective-permute-start(f32[3,2048]{1,0:T(4,128)S(1)} %get-tuple-element.60.message), channel_id=1, source_target_pairs={{0,1},{1,0},{2,3},{3,2},{4,5},{5,4},{6,7},{7,6},{8,9},{9,8},{10,11... | collective-permute-start | bytes 73736 | tf_op jit(solution)/shard_map/ppermute | solution.py:542
  60.7 7.9 %collective-permute-start.16 = (f32[3,2048]{1,0:T(4,128)S(1)}, f32[3,2048]{1,0:T(4,128)S(1)}, u32[]{:S(2)}, u32[]{:S(2)}) collective-permute-start(f32[3,2048]{1,0:T(4,128)S(1)} %shard_map.114), channel_id=1, source_target_pairs={{0,2},{2,4},{4,6},{6,0},{1,3},{3,5},{5,7},{7,1},{8,10},{10,12},{12... | collective-permute-start | bytes 73736 | tf_op jit(solution)/shard_map/ppermute | solution.py:547
  64.0 6.1 %collective-permute-start.15 = (f32[3,2048]{1,0:T(4,128)S(1)}, f32[3,2048]{1,0:T(4,128)S(1)}, u32[]{:S(2)}, u32[]{:S(2)}) collective-permute-start(f32[3,2048]{1,0:T(4,128)S(1)} %shard_map.114), channel_id=1, source_target_pairs={{0,4},{2,6},{4,0},{6,2},{1,5},{3,7},{5,1},{7,3},{8,12},{10,14},{12... | collective-permute-start | bytes 73736 | tf_op jit(solution)/shard_map/ppermute | solution.py:547
  67.9 3.9 %collective-permute-start.14 = (f32[3,2048]{1,0:T(4,128)S(1)}, f32[3,2048]{1,0:T(4,128)S(1)}, u32[]{:S(2)}, u32[]{:S(2)}) collective-permute-start(f32[3,2048]{1,0:T(4,128)S(1)} %shard_map.114), channel_id=1, source_target_pairs={{0,6},{2,0},{4,2},{6,4},{1,7},{3,1},{5,3},{7,5},{8,14},{10,8},{12,... | collective-permute-start | bytes 73736 | tf_op jit(solution)/shard_map/ppermute | solution.py:547
  77.1 10.1 %copy-start.1 = (bf16[512,2048]{1,0:T(8,128)(2,1)}, bf16[512,2048]{1,0:T(8,128)(2,1)S(1)}, u32[]{:S(2)}) copy-start(bf16[512,2048]{1,0:T(8,128)(2,1)S(1)} %get-tuple-element.72.d_values_in.d_values) | copy-start | bytes 6291460
  77.1 10.0 %collective-permute-start.20 = (bf16[512,2048]{1,0:T(8,128)(2,1)}, bf16[512,2048]{1,0:T(8,128)(2,1)S(1)}, u32[]{:S(2)}, u32[]{:S(2)}) collective-permute-start(bf16[512,2048]{1,0:T(8,128)(2,1)} %get-tuple-element.75), channel_id=1, source_target_pairs={{0,8},{8,0},{1,9},{9,1},{2,10},{10,2},{3,11},{11,3},{4,12},{12,4},... | collective-permute-start | bytes 6291464 | tf_op jit(solution)/shard_map/ppermute | solution.py:31
  84.0 5.1 %copy-start = (bf16[512,1024]{1,0:T(8,128)(2,1)}, bf16[512,1024]{1,0:T(8,128)(2,1)S(1)}, u32[]{:S(2)}) copy-start(bf16[512,1024]{1,0:T(8,128)(2,1)S(1)} %get-tuple-element.70.d_query_in.d) | copy-start | bytes 3145732
  85.2 3.8 %collective-permute-start.19 = (bf16[512,1024]{1,0:T(8,128)(2,1)S(1)}, bf16[512,1024]{1,0:T(8,128)(2,1)S(1)}, u32[]{:S(2)}, u32[]{:S(2)}) collective-permute-start(bf16[512,1024]{1,0:T(8,128)(2,1)S(1)} %shard_map.118), channel_id=1, source_target_pairs={{0,8},{8,0},{1,9},{9,1},{2,10},{10,2},{3,11},{11,3},{4,12},{12,4},... | collective-permute-start | bytes 3145736 | tf_op jit(solution)/shard_map/ppermute | solution.py:31
  87.1 3.3 %collective-permute-start.18 = (bf16[512,1024]{1,0:T(8,128)(2,1)S(1)}, bf16[512,1024]{1,0:T(8,128)(2,1)S(1)}, u32[]{:S(2)}, u32[]{:S(2)}) collective-permute-start(bf16[512,1024]{1,0:T(8,128)(2,1)S(1)} %shard_map.119), channel_id=1, source_target_pairs={{0,8},{8,0},{1,9},{9,1},{2,10},{10,2},{3,11},{11,3},{4,12},{12,4},... | collective-permute-start | bytes 3145736 | tf_op jit(solution)/shard_map/ppermute | solution.py:31
  154.6 43.2 %all-to-all-start.1 = ((bf16[32,8,4096]{2,1,0:T(8,128)(2,1)}), bf16[32,8,4096]{2,1,0:T(8,128)(2,1)S(1)}, u32[]{:S(2)}, u32[]{:S(2)}) async-start(bf16[32,8,4096]{2,1,0:T(8,128)(2,1)} %shard_map.123), calls=%async_computation.1 | async-start | bytes 4194304 | tf_op jit(solution)/shard_map/all_to_all | solution.py:599
  159.6 26.3 %collective-permute-start.17 = (bf16[1,1024]{1,0:T(2,128)(2,1)S(1)}, bf16[1,1024]{1,0:T(2,128)(2,1)S(1)}, u32[]{:S(2)}, u32[]{:S(2)}) collective-permute-start(bf16[1,1024]{1,0:T(2,128)(2,1)S(1)} %slice.31), channel_id=1, source_target_pairs={{1,0},{2,1},{3,2},{4,3},{5,4},{6,5},{7,6},{9,8},{10,9},{11,10},{12... | collective-permute-start | bytes 6152 | tf_op jit(solution)/shard_map/ppermute | solution.py:35
where the time goes:
time: 203 us; the launch traced here: 200 us
  blocking collectives  61 us (30%)
  Pallas kernels  56.4 us (28%)
  waiting for transfers between devices  47.3 us (23%)
  starting transfers between devices  26.1 us (13%)
  local copies, waits for them, and re-layouts  6.85 us (3%)
    all_to_all x1, blocking collectives, local_step(): lax.all_to_all(pair_sum.reshape(64, -1, pair_sum.shape[1]), ('xl', 'dp',...  61 us
    pallas_call x13, Pallas kernels, call(): pl.pallas_call(body, out_shape=[jax.ShapeDtypeStruct(s, t) for s, t in vm...  52.3 us
    ppermute x2, waiting for transfers between devices, along_ctx(): lax.ppermute(a, CTX, [(i, i + by) for i in range(RANGES) if 0 <= i + by <...  29.5 us
    ppermute x4, waiting for transfers between devices, along_x(): return lax.ppermute(a, ('xl', 'xh'), pairs)  12.6 us
    ppermute x3, starting transfers between devices, local_step(): lax.ppermute(pair, 'z', [(i, (i - d) % 4) for i in range(4)])  7.85 us
    all_to_all x1, starting transfers between devices, local_step(): lax.all_to_all(sum_ranks(exchanged, 32), ('dp', 'z', 'xh'), 0, 0, tiled=T...  5.01 us
    unnamed x32, local copies, waits for them, and re-layouts  4.21 us
  transfers between devices with their start and end apart: 22, of which 8 were waited for; matrix products, arithmetic and copies ran while one was open for 2% of the time, Pallas kernels for 19%

commit v1 on v0

--- a/solution.py
+++ b/solution.py
@@ -86,11 +86,20 @@
     return pl.ds(pl.multiple_of(index * depth, depth), depth)
 
 
+def turn(core, tok, turned):
+    rows = tok.shape[1] // 4
+    for b in range(2):
+        for c in range(2):
+            start = pl.multiple_of((core ^ c) * 2 * rows + b * rows, rows)
+            first = (2 * b + c) * rows
+            turned[pl.ds(start, rows), :] = tok[:, first : first + rows].T
+
+
 def near_kernel(place, tok, q0, q1, queries, turned, wq, q_sems):
     loads = fetch_panel(place, (q0, q1), wq, q_sems)
     for c in loads:
         c.start()
-    turned[...] = tok[...].T
+    turn(place[0] % 2, tok, turned)
     for c in loads:
         c.wait()
     queries[...] = mxu(tok[:, panel_columns(place[0] // 2, wq.shape[0])], wq[...])
@@ -102,7 +111,7 @@
     loads = fetch_panel(place, (u0, u1, u2, u3), wu, sems)
     for c in loads:
         c.start()
-    turned_prev[...] = tok_prev[...].T
+    turn(place[0] % 2, tok_prev, turned_prev)
     for c in loads:
         c.wait()
     values[...] = mxu(tok[:, panel_columns(place[0] // 2, wu.shape[0])], wu[...])
@@ -163,11 +172,11 @@
         stats_out[rows, :] = stats
         outs[pl.ds(n, 1), :] = carry[0:1, :]
         total = jnp.exp(keep[SPAN - 1 : SPAN, :])
-        upper = sub <= lane
+        mask = jnp.where(sub <= lane, 0.0, -1e30)
         for h in range(heads):
             cols = head_cols(h)
             gap = keep_rows[h : h + 1, :] - keep[:, h : h + 1]
-            band = jnp.where(upper, jnp.exp(jnp.where(upper, gap, 0.0)), 0.0)
+            band = jnp.exp(gap + mask)
             local = mxu(band.astype(BF16), cot[rows, cols])
             adjoint[rows, cols] = local
             d = total[:, h : h + 1]
@@ -198,13 +207,13 @@
         rows = span(n)
         mix, keep = mix_ref[rows, :], keep_ref[rows, :]
         keep_rows = keep.T
-        lower = ids((SPAN, LANES), 0) >= ids((SPAN, LANES), 1)
+        mask = jnp.where(ids((SPAN, LANES), 0) >= ids((SPAN, LANES), 1), 0.0, -1e30)
         ins[pl.ds(n, 1), :] = carry[0:1, :]
         total = jnp.exp(keep[SPAN - 1 : SPAN, :])
         for h in range(heads):
             cols = head_cols(h)
             gap = keep[:, h : h + 1] - keep_rows[h : h + 1, :]
-            band = jnp.where(lower, jnp.exp(jnp.where(lower, gap, 0.0)), 0.0)
+            band = jnp.exp(gap + mask)
             band = band.astype(BF16)
             added, rest = halves(mix[:, h : h + 1] * values[rows, cols])
             local = mxu(band, added) + mxu(band, rest)
@@ -240,21 +249,13 @@
     return chain(place[2] == 1, other, incoming, 2)
 
 
-def side_rows(core, turned, b):
-    rows = turned.shape[0] // 4
-    return turned[pl.ds(pl.multiple_of((2 * b + core) * rows, rows), rows), :]
-
-
-def shares(core, turned, d, share, share_out, sems):
+def shares(turned, d, share, share_out, sems):
     step = 512
     saves = []
-    rows = share.shape[0] // 2
+    rows = share.shape[0]
     for i in range(d.shape[1] // step):
         part = slice(i * step, (i + 1) * step)
-        for b in range(2):
-            share[b * rows : (b + 1) * rows, part] = mxu(
-                side_rows(core, turned, b), d[:, part]
-            ).astype(BF16)
+        share[:, part] = mxu(turned[rows:, :], d[:, part]).astype(BF16)
         saves.append(whole_copy(share.at[:, part], share_out.at[:, part], sems.at[i]))
         saves[i].start()
     return saves
@@ -287,7 +288,7 @@
         return after + last
 
     lax.fori_loop(0, blocks, block, jnp.zeros((1, LANES), F32))
-    saves = shares(1 - place[0] % 2, turned, d_values, share, share_out, s_sems)
+    saves = shares(turned, d_values, share, share_out, s_sems)
     for c in saves:
         c.wait()
 
@@ -336,35 +337,22 @@
         block_copy(dechunked, dechunked_out, d_sems, n).wait()
 
 
-def share_kernel(place, turned, d, share):
+def share_kernel(turned, d, share):
     step = 512
-    rows = share.shape[0] // 2
+    rows = share.shape[0]
     for i in range(d.shape[1] // step):
         part = slice(i * step, (i + 1) * step)
-        for b in range(2):
-            share[b * rows : (b + 1) * rows, part] = mxu(
-                side_rows(1 - place[0] % 2, turned, b), d[:, part]
-            ).astype(BF16)
-
-
-def up_sum_kernel(place, d_values, theirs, turned, out):
-    add_share(place, turned, d_values, theirs, out, out.shape[1] - d_values.shape[1])
-
-
-def route_sum_kernel(place, d, theirs, partial, turned, out, *, at):
-    add_share(place, turned, d, theirs, out, at)
-
-
-def add_share(place, turned, d, theirs, out, at):
+        share[:, part] = mxu(turned[rows:, :], d[:, part]).astype(BF16)
+
+
+def sum_share_kernel(d, theirs, turned, *refs, at):
+    out = refs[-1]
     step = 512
-    rows = theirs.shape[0] // 2
+    rows = theirs.shape[0]
     for i in range(d.shape[1] // step):
         part = slice(i * step, (i + 1) * step)
-        for b in range(2):
-            half = slice(b * rows, (b + 1) * rows)
-            mine = mxu(side_rows(place[0] % 2, turned, b), d[:, part])
-            total = mine + theirs[half, part].astype(F32)
-            out[half, at + i * step : at + (i + 1) * step] = total.astype(BF16)
+        total = mxu(turned[0:rows, :], d[:, part]) + theirs[:, part].astype(F32)
+        out[:, at + i * step : at + (i + 1) * step] = total.astype(BF16)
 
 
 def tokens_kernel(place, d_query_in, d_key_in, d_values_in, *refs):
@@ -459,10 +447,6 @@
 DMA = pltpu.SemaphoreType.DMA
 
 
-def in_hbm(a):
-    return pltpu.with_memory_space_constraint(a, pltpu.HBM)
-
-
 def call(
     body, place, vmem_args, hbm_args, vmem_outs, hbm_outs, scratch, flops, limit, aliases=None
 ):
@@ -470,13 +454,15 @@
         body,
         out_shape=[jax.ShapeDtypeStruct(s, t) for s, t in vmem_outs]
         + [pltpu.HBM(s, t) for s, t in hbm_outs],
-        in_specs=[SMEM] + [VMEM] * len(vmem_args) + [HBM] * len(hbm_args),
+        in_specs=([] if place is None else [SMEM])
+        + [VMEM] * len(vmem_args)
+        + [HBM] * len(hbm_args),
         out_specs=[VMEM] * len(vmem_outs) + [HBM] * len(hbm_outs),
         scratch_shapes=scratch,
         input_output_aliases=aliases or {},
         cost_estimate=pl.CostEstimate(flops=flops, bytes_accessed=1 << 20, transcendentals=0),
         compiler_params=pltpu.CompilerParams(vmem_limit_bytes=limit << 20),
-    )(place, *vmem_args, *[in_hbm(a) for a in hbm_args])
+    )(*(() if place is None else (place,)), *vmem_args, *hbm_args)
 
 
 def local_step(tokens, bounds, decay_rates, w_query, w_key, w_up, grad_out):
@@ -570,29 +556,28 @@
     )
     after = along_ctx(d_prev[:1], -1)
     (q_share,) = call(
-        share_kernel, place, (turned, d_query), (), ((half_flat, BF16),), (), [], 500_000_000, 6
+        share_kernel, None, (turned, d_query), (), ((half_flat, BF16),), (), [], 500_000_000, 6
     )
     q_theirs = swap_core(q_share)
     d_prev_late, q_share = lax.optimization_barrier((d_prev, q_share))
     (k_share,) = call(
-        share_kernel, place, (turned_prev, d_prev_late), (), ((half_flat, BF16),), (), [],
+        share_kernel, None, (turned_prev, d_prev_late), (), ((half_flat, BF16),), (), [],
         500_000_000, 6,
     )
     k_theirs = swap_core(k_share)
     full = (2 * rows, 2 * width + hidden)
-    (partial,) = call(
-        up_sum_kernel, place,
-        (d_values, up_theirs, turned), (), ((full, BF16),), (), [], 1_500_000_000, 8,
-    )
-    sums = partial
+    sums = ()
     for d, theirs, lhs, at in (
-        (d_query, q_theirs, turned, 0), (d_prev, k_theirs, turned_prev, width)
+        (d_values, up_theirs, turned, 2 * width),
+        (d_query, q_theirs, turned, 0),
+        (d_prev, k_theirs, turned_prev, width),
     ):
-        (sums,) = call(
-            functools.partial(route_sum_kernel, at=at), place,
-            (d, theirs, sums, lhs), (), ((full, BF16),), (), [], 700_000_000, 8, {3: 0},
+        sums = call(
+            functools.partial(sum_share_kernel, at=at), None,
+            (d, theirs, lhs, *sums), (), ((full, BF16),), (), [], 700_000_000, 8,
+            {3: 0} if sums else None,
         )
-    pair_sum = sums
+    (pair_sum,) = sums
     exchanged = lax.all_to_all(
         pair_sum.reshape(64, -1, pair_sum.shape[1]), ("xl", "dp", "z", "xh"), 0, 0, tiled=True
     )

time: 203 us -> 196 us (0.966)
  Pallas kernels: 56.4 us -> 50.8 us
  local copies, waits for them, and re-layouts: 6.85 us -> 1.7 us
  waiting for transfers between devices: 47.3 us -> 52 us
    pallas_call x13, Pallas kernels: 52.3 us -> 46.7 us  [call(): pl.pallas_call(body, out_shape=[jax.ShapeDtypeStruct(s, t) for s, t in vm...]
    unnamed x32 -> x38, local copies, waits for them, and re-layouts: 4.21 us -> 0.09 us
    ppermute x4, waiting for transfers between devices: 12.6 us -> 16.5 us  [along_x(): return lax.ppermute(a, ('xl', 'xh'), pairs)]
  transfers between devices with their start and end apart: 22 -> 22, of which waited for: 8 -> 10; matrix products, arithmetic and copies ran while one was open for 2% -> 2% of each run, Pallas kernels for 19% -> 17%
where the time goes in v1:
time: 196 us; the launch traced here: 195 us
  blocking collectives  60.8 us (31%)
  waiting for transfers between devices  52 us (27%)
  Pallas kernels  50.8 us (26%)
  starting transfers between devices  27.1 us (14%)
    all_to_all x1, blocking collectives, local_step(): lax.all_to_all(pair_sum.reshape(64, -1, pair_sum.shape[1]), ('xl', 'dp',...  60.8 us
    pallas_call x13, Pallas kernels, call(): pl.pallas_call(body, out_shape=[jax.ShapeDtypeStruct(s, t) for s, t in vm...  46.7 us
    ppermute x2, waiting for transfers between devices, along_ctx(): lax.ppermute(a, CTX, [(i, i + by) for i in range(RANGES) if 0 <= i + by <...  29.4 us
    ppermute x4, waiting for transfers between devices, along_x(): return lax.ppermute(a, ('xl', 'xh'), pairs)  16.5 us
    ppermute x3, starting transfers between devices, local_step(): lax.ppermute(pair, 'z', [(i, (i - d) % 4) for i in range(4)])  7.85 us
    all_to_all x1, starting transfers between devices, local_step(): lax.all_to_all(sum_ranks(exchanged, 32), ('dp', 'z', 'xh'), 0, 0, tiled=T...  5.95 us
  transfers between devices with their start and end apart: 22, of which 10 were waited for; matrix products, arithmetic and copies ran while one was open for 2% of the time, Pallas kernels for 17%

profile of v1, /device:TPU:0, one launch (start us, length us, event | category | flops | bytes accessed | tf_op | source)
XLA Modules:
  0.0 195.2 jit_solution(5056170029147394893)
XLA Ops:
  0.6 0.0 copy-start.7
  0.7 0.1 collective-permute-start.1
  0.8 2.9 %collective-permute-start.2 = (bf16[256,1024]{1,0:T(8,128)(2,1)}, bf16[256,1024]{1,0:T(8,128)(2,1)}, u32[]{:S(2)}, u32[]{:S(2)}) collective-permute-start(bf16[256,1024]{1,0:T(8,128)(2,1)} %refs_0_.1), channel_id=1, source_target_pairs={{0,17},{1,16},{16,0},{17,1},{2,19},{3,18},{18,2},{19,3},{4,21},{5,... | collective-permute-start | bytes 1572872 | tf_op jit(solution)/shard_map/ppermute | solution.py:27
  3.7 0.1 collective-permute-start.5
  3.8 0.0 collective-permute-start.3
  3.8 1.3 fusion
  5.1 0.8 collective-permute-start.8
  6.0 0.1 pad_add_fusion.place
  6.0 0.0 collective-permute-done.1.q1.refs_1_
  6.1 1.7 shard_map.110
  7.8 8.0 %collective-permute-done.2.q2.refs_2_ = bf16[256,1024]{1,0:T(8,128)(2,1)} collective-permute-done((bf16[256,1024]{1,0:T(8,128)(2,1)}, bf16[256,1024]{1,0:T(8,128)(2,1)}, u32[]{:S(2)}, u32[]{:S(2)}) %collective-permute-start.2) | collective-permute-done | bytes 524320 | tf_op jit(solution)/shard_map/ppermute | solution.py:27
  15.8 4.4 %collective-permute-done.3.k2.refs_6_ = bf16[256,1024]{1,0:T(8,128)(2,1)} collective-permute-done((bf16[256,1024]{1,0:T(8,128)(2,1)}, bf16[256,1024]{1,0:T(8,128)(2,1)}, u32[]{:S(2)}, u32[]{:S(2)}) %collective-permute-start.3) | collective-permute-done | bytes 524320 | tf_op jit(solution)/shard_map/ppermute | solution.py:27
  20.2 0.0 collective-permute-start.4
  20.2 0.5 collective-permute-start.6
  20.7 0.0 copy-start.6
  20.7 0.0 copy-start.8
  20.7 0.0 copy-start.17
  20.7 1.6 collective-permute-start
  22.4 0.1 slice_bitcast_fusion
  22.4 4.9 %collective-permute-done = bf16[1,1024]{1,0:T(2,128)(2,1)S(1)} collective-permute-done((bf16[1,1024]{1,0:T(2,128)(2,1)S(1)}, bf16[1,1024]{1,0:T(2,128)(2,1)S(1)}, u32[]{:S(2)}, u32[]{:S(2)}) %collective-permute-start) | collective-permute-done | bytes 2080 | tf_op jit(solution)/shard_map/ppermute | solution.py:35
  27.4 0.1 collective-permute-start.7
  27.5 0.3 pad_maximum_fusion.tok_prev
  27.8 0.1 collective-permute-start.9
  27.9 0.0 collective-permute-done.4.q3.refs_3_
  27.9 0.5 collective-permute-start.10
  28.4 0.0 collective-permute-done.6.k3.refs_7_
  28.4 8.4 %shard_map.111 = (f32[512,1024]{1,0:T(8,128)S(1)}, f32[512,1024]{1,0:T(8,128)S(1)}, f32[512,2048]{1,0:T(8,128)S(1)}, f32[512,128]{1,0:T(8,128)S(1)}, f32[512,128...) custom-call(s32[3]{0:T(128)S(1)} %pad_add_fusion.place, ...), custom_call_target="tpu_custom_call" | custom-call | flops 6000000000 | bytes 1048576 | tf_op jit(solution)/shard_map/pallas_call | solution.py:453
  36.8 0.0 collective-permute-done.8.u5.refs_13_
  36.9 4.1 %collective-permute-done.7.u4.refs_12_ = bf16[128,2048]{1,0:T(8,128)(2,1)S(1)} collective-permute-done((bf16[128,2048]{1,0:T(8,128)(2,1)S(1)}, bf16[128,2048]{1,0:T(8,128)(2,1)S(1)}, u32[]{:S(2)}, u32[]{:S(2)}) %collective-permute-start.7) | collective-permute-done | bytes 524320 | tf_op jit(solution)/shard_map/ppermute | solution.py:27
  41.0 0.5 collective-permute-start.12
  41.5 0.0 collective-permute-done.9.u2.refs_10_
  41.5 0.0 collective-permute-done.10.u3.refs_11_
  41.5 2.3 %shard_map.112 = (f32[512,2048]{1,0:T(8,128)S(1)}, bf16[1024,512]{1,0:T(8,128)(2,1)S(1)}) custom-call(s32[3]{0:T(128)S(1)} %pad_add_fusion.place, bf16[512,1024]{1,0:T(8,128)(2,1)S(1)} %bitcast.17, bf16[512,1024]{1,0:T(8,128)(2,1)S(1)} %pad_maximum_fusion.tok_prev, bf16[128,2048]{1,0:T(8,128)(2,1)S(1)} %get-tuple-element.53.u0.refs_8_, ...), custom_call_target="tpu_custom_call" | custom-call | flops 2000000000 | bytes 1048576 | tf_op jit(solution)/shard_map/pallas_call | solution.py:453
  43.9 6.6 %shard_map.113 = (f32[512,2048]{1,0:T(8,128)S(1)}, f32[512,2048]{1,0:T(8,128)S(1)}, f32[4,2048]{1,0:T(4,128)S(1)}, f32[3,2048]{1,0:T(4,128)S(1)}) custom-call(s32[3]{0:T(128)S(1)} %pad_add_fusion.place, f32[512,128]{1,0:T(8,128)S(1)} %get-tuple-element.49.mix_ref, f32[512,128]{1,0:T(8,128)S(1)} %get-tuple-element.51.keep_ref, ...), custom_call_target="tpu_custom_call" | custom-call | flops 6000000000 | bytes 1048576 | tf_op jit(solution)/shard_map/pallas_call | solution.py:453
  50.5 3.8 %collective-permute-start.13 = (f32[3,2048]{1,0:T(4,128)S(1)}, f32[3,2048]{1,0:T(4,128)S(1)}, u32[]{:S(2)}, u32[]{:S(2)}) collective-permute-start(f32[3,2048]{1,0:T(4,128)S(1)} %get-tuple-element.60.message), channel_id=1, source_target_pairs={{0,1},{1,0},{2,3},{3,2},{4,5},{5,4},{6,7},{7,6},{8,9},{9,8},{10,11... | collective-permute-start | bytes 73736 | tf_op jit(solution)/shard_map/ppermute | solution.py:528
  54.3 1.9 collective-permute-done.13.other
  56.2 0.6 shard_map.114
  56.8 3.3 %collective-permute-start.16 = (f32[3,2048]{1,0:T(4,128)S(1)}, f32[3,2048]{1,0:T(4,128)S(1)}, u32[]{:S(2)}, u32[]{:S(2)}) collective-permute-start(f32[3,2048]{1,0:T(4,128)S(1)} %shard_map.114), channel_id=1, source_target_pairs={{0,2},{2,4},{4,6},{6,0},{1,3},{3,5},{5,7},{7,1},{8,10},{10,12},{12... | collective-permute-start | bytes 73736 | tf_op jit(solution)/shard_map/ppermute | solution.py:533
  60.0 3.9 %collective-permute-start.15 = (f32[3,2048]{1,0:T(4,128)S(1)}, f32[3,2048]{1,0:T(4,128)S(1)}, u32[]{:S(2)}, u32[]{:S(2)}) collective-permute-start(f32[3,2048]{1,0:T(4,128)S(1)} %shard_map.114), channel_id=1, source_target_pairs={{0,4},{2,6},{4,0},{6,2},{1,5},{3,7},{5,1},{7,3},{8,12},{10,14},{12... | collective-permute-start | bytes 73736 | tf_op jit(solution)/shard_map/ppermute | solution.py:533
  63.9 0.7 collective-permute-start.14
  64.6 1.5 collective-permute-done.15.next2
  66.2 1.7 collective-permute-done.14.next1
  67.8 5.3 %shard_map.115 = (bf16[512,2048]{1,0:T(8,128)(2,1)S(1)}, f32[4,2048]{1,0:T(4,128)S(1)}, bf16[512,2048]{1,0:T(8,128)(2,1)}) custom-call(s32[3]{0:T(128)S(1)} %pad_add_fusion.place, f32[4,2048]{1,0:T(4,128)S(1)} %get-tuple-element.59.outs, f32[512,128]{1,0:T(8,128)S(1)} %get-tuple-element.49.mix_ref, f32[512,128]{1,0:T(8,128)S(1)} %get-tuple-element.51.keep_ref, ...), custom_call_target="tpu_custom_call" | custom-call | flops 3000000000 | bytes 1048576 | tf_op jit(solution)/shard_map/pallas_call | solution.py:453
  73.1 0.1 collective-permute-start.20
  73.2 6.8 %shard_map.116 = (bf16[512,1024]{1,0:T(8,128)(2,1)S(1)}, bf16[512,1024]{1,0:T(8,128)(2,1)S(1)}, bf16[512,2048]{1,0:T(8,128)(2,1)}) custom-call(s32[3]{0:T(128)S(1)} %pad_add_fusion.place, f32[4,2048]{1,0:T(4,128)S(1)} %get-tuple-element.58.ins, f32[4,2048]{1,0:T(4,128)S(1)} %get-tuple-element.63.tails, f32[512,128]{1,0:T(8,128)S(1)} %get-tuple-element.51.keep_ref, ...), custom_call_target="tpu_custom_call" | custom-call | flops 3000000000 | bytes 1048576 | tf_op jit(solution)/shard_map/pallas_call | solution.py:453
  80.0 0.0 copy-start
  80.0 0.7 shard_map.118
  80.8 0.6 collective-permute-start.19
  81.3 0.7 shard_map.119
  82.0 0.1 collective-permute-start.18
  82.1 1.3 shard_map.120.refs_0_
  83.4 0.2 collective-permute-done.19.theirs
  83.6 0.7 shard_map.121.refs_0_
  84.3 0.8 collective-permute-done.18.theirs
  85.1 0.7 shard_map.122
  85.8 60.8 %all_to_all.10.parts = bf16[64,8,4096]{2,1,0:T(8,128)(2,1)S(1)} all-to-all(bf16[64,8,4096]{2,1,0:T(8,128)(2,1)S(1)} %bitcast.14), channel_id=1, replica_groups=mesh['dp'=4,'xl'=2,'core'=2,'z'=4,'xh'=2] {'xl','dp','z','xh'}, dimensions={0} | all-to-all | bytes 8388608 | tf_op jit(solution)/shard_map/all_to_all | solution.py:581
  146.7 2.0 %shard_map.123 = bf16[32,8,4096]{2,1,0:T(8,128)(2,1)} custom-call(bf16[64,8,4096]{2,1,0:T(8,128)(2,1)S(1)} %all_to_all.10.parts), custom_call_target="tpu_custom_call" | custom-call | tf_op jit(solution)/shard_map/pallas_call | solution.py:400
  148.7 5.9 %all-to-all-start.1 = ((bf16[32,8,4096]{2,1,0:T(8,128)(2,1)}), bf16[32,8,4096]{2,1,0:T(8,128)(2,1)S(1)}, u32[]{:S(2)}, u32[]{:S(2)}) async-start(bf16[32,8,4096]{2,1,0:T(8,128)(2,1)} %shard_map.123), calls=%async_computation.1 | async-start | bytes 4194304 | tf_op jit(solution)/shard_map/all_to_all | solution.py:584
  154.6 1.5 collective-permute-start.17
  156.2 0.3 slice.30
  156.4 24.5 %collective-permute-done.17 = bf16[1,1024]{1,0:T(2,128)(2,1)S(1)} collective-permute-done((bf16[1,1024]{1,0:T(2,128)(2,1)S(1)}, bf16[1,1024]{1,0:T(2,128)(2,1)S(1)}, u32[]{:S(2)}, u32[]{:S(2)}) %collective-permute-start.17) | collective-permute-done | bytes 2080 | tf_op jit(solution)/shard_map/ppermute | solution.py:35
  180.9 1.1 pad_maximum_fusion.1.d_key_in
  182.0 10.9 %shard_map.117 = bf16[512,1024]{1,0:T(8,128)(2,1)} custom-call(s32[3]{0:T(128)} %copy-done.5, bf16[512,1024]{1,0:T(8,128)(2,1)} %copy-done, bf16[512,1024]{1,0:T(8,128)(2,1)} %pad_maximum_fusion.1.d_key_in, bf16[512,2048]{1,0:T(8,128)(2,1)} %copy-done.1, bf16[256,1024]{1,0:T(8,128)(2,1)} %refs_0_.1, bf16[256,1024]{1,0:T(8,128)(2,1)} %copy-done.9, ...), custom_call_target="tpu_custom_call" | custom-call | flops 5000000000 | bytes 1048576 | tf_op jit(solution)/shard_map/pallas_call | solution.py:453
  192.9 2.1 %shard_map.124 = (f32[256,1024]{1,0:T(8,128)}, f32[256,1024]{1,0:T(8,128)}, f32[256,2048]{1,0:T(8,128)}) custom-call(bf16[32,8,4096]{2,1,0:T(8,128)(2,1)S(1)} %all-to-all-done.1.parts), custom_call_target="tpu_custom_call" | custom-call | tf_op jit(solution)/shard_map/pallas_call | solution.py:434
  (43 shorter events, 0.1 us)
Async XLA Ops:
  0.6 5.4 %copy-start.7 = (bf16[256,1024]{1,0:T(8,128)(2,1)S(1)}, bf16[256,1024]{1,0:T(8,128)(2,1)}, u32[]{:S(2)}) copy-start(bf16[256,1024]{1,0:T(8,128)(2,1)} %refs_0_.1) | copy-start | bytes 1572868
  0.6 5.3 %copy-start.18 = (f32[16]{0:T(128)S(1)}, f32[16]{0:T(128)}, u32[]{:S(2)}) copy-start(f32[16]{0:T(128)} %param.9) | copy-start | bytes 196
  0.7 5.4 %copy-start.2 = (bf16[1,512,1024]{2,1,0:T(8,128)(2,1)S(1)}, bf16[1,512,1024]{2,1,0:T(8,128)(2,1)}, u32[]{:S(2)}) copy-start(bf16[1,512,1024]{2,1,0:T(8,128)(2,1)} %param.7) | copy-start | bytes 3145732
  0.7 5.4 %collective-permute-start.1 = (bf16[256,1024]{1,0:T(8,128)(2,1)}, bf16[256,1024]{1,0:T(8,128)(2,1)S(1)}, u32[]{:S(2)}, u32[]{:S(2)}) collective-permute-start(bf16[256,1024]{1,0:T(8,128)(2,1)} %refs_0_.1), channel_id=1, source_target_pairs={{0,8},{8,0},{1,9},{9,1},{2,10},{10,2},{3,11},{11,3},{4,12},{12,4},... | collective-permute-start | bytes 1572872 | tf_op jit(solution)/shard_map/ppermute | solution.py:31
  0.8 15.0 %collective-permute-start.2 = (bf16[256,1024]{1,0:T(8,128)(2,1)}, bf16[256,1024]{1,0:T(8,128)(2,1)}, u32[]{:S(2)}, u32[]{:S(2)}) collective-permute-start(bf16[256,1024]{1,0:T(8,128)(2,1)} %refs_0_.1), channel_id=1, source_target_pairs={{0,17},{1,16},{16,0},{17,1},{2,19},{3,18},{18,2},{19,3},{4,21},{5,... | collective-permute-start | bytes 1572872 | tf_op jit(solution)/shard_map/ppermute | solution.py:27
  3.7 24.1 %collective-permute-start.5 = (bf16[256,1024]{1,0:T(8,128)(2,1)}, bf16[256,1024]{1,0:T(8,128)(2,1)}, u32[]{:S(2)}, u32[]{:S(2)}) collective-permute-start(bf16[256,1024]{1,0:T(8,128)(2,1)} %refs_4_.1), channel_id=1, source_target_pairs={{0,8},{8,0},{1,9},{9,1},{2,10},{10,2},{3,11},{11,3},{4,12},{12,4},... | collective-permute-start | bytes 1572872 | tf_op jit(solution)/shard_map/ppermute | solution.py:31
  3.8 16.3 %collective-permute-start.3 = (bf16[256,1024]{1,0:T(8,128)(2,1)}, bf16[256,1024]{1,0:T(8,128)(2,1)}, u32[]{:S(2)}, u32[]{:S(2)}) collective-permute-start(bf16[256,1024]{1,0:T(8,128)(2,1)} %refs_4_.1), channel_id=1, source_target_pairs={{0,16},{1,17},{16,1},{17,0},{2,18},{3,19},{18,3},{19,2},{4,20},{5,... | collective-permute-start | bytes 1572872 | tf_op jit(solution)/shard_map/ppermute | solution.py:27
  5.1 36.4 %copy-start.3 = (bf16[128,2048]{1,0:T(8,128)(2,1)}, bf16[128,2048]{1,0:T(8,128)(2,1)S(1)}, u32[]{:S(2)}) copy-start(bf16[128,2048]{1,0:T(8,128)(2,1)S(1)} %get-tuple-element.54.u1.refs_9_) | copy-start | bytes 1572868
  5.1 36.4 %copy-start.4 = (bf16[128,2048]{1,0:T(8,128)(2,1)}, bf16[128,2048]{1,0:T(8,128)(2,1)S(1)}, u32[]{:S(2)}) copy-start(bf16[128,2048]{1,0:T(8,128)(2,1)S(1)} %get-tuple-element.53.u0.refs_8_) | copy-start | bytes 1572868
  5.1 31.7 %collective-permute-start.8 = (bf16[128,2048]{1,0:T(8,128)(2,1)S(1)}, bf16[128,2048]{1,0:T(8,128)(2,1)}, u32[]{:S(2)}, u32[]{:S(2)}) collective-permute-start(bf16[128,2048]{1,0:T(8,128)(2,1)S(1)} %get-tuple-element.54.u1.refs_9_), channel_id=1, source_target_pairs={{0,16},{1,17},{16,1},{17,0},{2,18},{3,19},{18,3},{19,2},{4,20},{5,... | collective-permute-start | bytes 1572872 | tf_op jit(solution)/shard_map/ppermute | solution.py:27
  6.0 67.2 %copy-start.5 = (s32[3]{0:T(128)}, s32[3]{0:T(128)S(1)}, u32[]{:S(2)}) copy-start(s32[3]{0:T(128)S(1)} %pad_add_fusion.place) | copy-start | bytes 40
  6.1 16.4 %copy-start.9 = (bf16[256,1024]{1,0:T(8,128)(2,1)}, bf16[256,1024]{1,0:T(8,128)(2,1)S(1)}, u32[]{:S(2)}) copy-start(bf16[256,1024]{1,0:T(8,128)(2,1)S(1)} %collective-permute-done.1.q1.refs_1_) | copy-start | bytes 1572868
  20.2 7.7 %collective-permute-start.4 = (bf16[256,1024]{1,0:T(8,128)(2,1)}, bf16[256,1024]{1,0:T(8,128)(2,1)S(1)}, u32[]{:S(2)}, u32[]{:S(2)}) collective-permute-start(bf16[256,1024]{1,0:T(8,128)(2,1)} %collective-permute-done.2.q2.refs_2_), channel_id=1, source_target_pairs={{0,8},{8,0},{1,9},{9,1},{2,10},{10,2},{3,11},{11,3},{4,12},{12,4},... | collective-permute-start | bytes 1572872 | tf_op jit(solution)/shard_map/ppermute | solution.py:31
  20.2 8.2 %collective-permute-start.6 = (bf16[256,1024]{1,0:T(8,128)(2,1)}, bf16[256,1024]{1,0:T(8,128)(2,1)S(1)}, u32[]{:S(2)}, u32[]{:S(2)}) collective-permute-start(bf16[256,1024]{1,0:T(8,128)(2,1)} %collective-permute-done.3.k2.refs_6_), channel_id=1, source_target_pairs={{0,8},{8,0},{1,9},{9,1},{2,10},{10,2},{3,11},{11,3},{4,12},{12,4},... | collective-permute-start | bytes 1572872 | tf_op jit(solution)/shard_map/ppermute | solution.py:31
  20.7 7.7 %copy-start.6 = (bf16[1,512,2048]{2,1,0:T(8,128)(2,1)S(1)}, bf16[1,512,2048]{2,1,0:T(8,128)(2,1)}, u32[]{:S(2)}) copy-start(bf16[1,512,2048]{2,1,0:T(8,128)(2,1)} %param.13) | copy-start | bytes 6291460
  20.7 7.7 %copy-start.8 = (bf16[256,1024]{1,0:T(8,128)(2,1)S(1)}, bf16[256,1024]{1,0:T(8,128)(2,1)}, u32[]{:S(2)}) copy-start(bf16[256,1024]{1,0:T(8,128)(2,1)} %refs_4_.1) | copy-start | bytes 1572868
  20.7 7.7 %copy-start.17 = (s32[1,512]{1,0:T(1,128)S(1)}, s32[1,512]{1,0:T(1,128)}, u32[]{:S(2)}) copy-start(s32[1,512]{1,0:T(1,128)} %bounds.1) | copy-start | bytes 6148
  20.7 6.6 %collective-permute-start = (bf16[1,1024]{1,0:T(2,128)(2,1)S(1)}, bf16[1,1024]{1,0:T(2,128)(2,1)S(1)}, u32[]{:S(2)}, u32[]{:S(2)}) collective-permute-start(bf16[1,1024]{1,0:T(2,128)(2,1)S(1)} %slice_bitcast_fusion.1), channel_id=1, source_target_pairs={{0,1},{1,2},{2,3},{3,4},{4,5},{5,6},{6,7},{8,9},{9,10},{10,11},{11... | collective-permute-start | bytes 6152 | tf_op jit(solution)/shard_map/ppermute | solution.py:35
  27.4 13.6 %collective-permute-start.7 = (bf16[128,2048]{1,0:T(8,128)(2,1)S(1)}, bf16[128,2048]{1,0:T(8,128)(2,1)S(1)}, u32[]{:S(2)}, u32[]{:S(2)}) collective-permute-start(bf16[128,2048]{1,0:T(8,128)(2,1)S(1)} %get-tuple-element.53.u0.refs_8_), channel_id=1, source_target_pairs={{0,17},{1,16},{16,0},{17,1},{2,19},{3,18},{18,2},{19,3},{4,21},{5,... | collective-permute-start | bytes 1572872 | tf_op jit(solution)/shard_map/ppermute | solution.py:27
  27.8 13.7 %collective-permute-start.9 = (bf16[128,2048]{1,0:T(8,128)(2,1)S(1)}, bf16[128,2048]{1,0:T(8,128)(2,1)S(1)}, u32[]{:S(2)}, u32[]{:S(2)}) collective-permute-start(bf16[128,2048]{1,0:T(8,128)(2,1)S(1)} %get-tuple-element.53.u0.refs_8_), channel_id=1, source_target_pairs={{0,8},{8,0},{1,9},{9,1},{2,10},{10,2},{3,11},{11,3},{4,12},{12,4},... | collective-permute-start | bytes 1572872 | tf_op jit(solution)/shard_map/ppermute | solution.py:31
  27.9 9.0 %copy-start.10 = (bf16[256,1024]{1,0:T(8,128)(2,1)}, bf16[256,1024]{1,0:T(8,128)(2,1)S(1)}, u32[]{:S(2)}) copy-start(bf16[256,1024]{1,0:T(8,128)(2,1)S(1)} %collective-permute-done.4.q3.refs_3_) | copy-start | bytes 1572868
  27.9 13.6 %collective-permute-start.10 = (bf16[128,2048]{1,0:T(8,128)(2,1)S(1)}, bf16[128,2048]{1,0:T(8,128)(2,1)S(1)}, u32[]{:S(2)}, u32[]{:S(2)}) collective-permute-start(bf16[128,2048]{1,0:T(8,128)(2,1)S(1)} %get-tuple-element.54.u1.refs_9_), channel_id=1, source_target_pairs={{0,8},{8,0},{1,9},{9,1},{2,10},{10,2},{3,11},{11,3},{4,12},{12,4},... | collective-permute-start | bytes 1572872 | tf_op jit(solution)/shard_map/ppermute | solution.py:31
  28.4 8.5 %copy-start.11 = (bf16[256,1024]{1,0:T(8,128)(2,1)}, bf16[256,1024]{1,0:T(8,128)(2,1)S(1)}, u32[]{:S(2)}) copy-start(bf16[256,1024]{1,0:T(8,128)(2,1)S(1)} %collective-permute-done.6.k3.refs_7_) | copy-start | bytes 1572868
  41.0 2.9 %copy-start.12 = (bf16[128,2048]{1,0:T(8,128)(2,1)}, bf16[128,2048]{1,0:T(8,128)(2,1)S(1)}, u32[]{:S(2)}) copy-start(bf16[128,2048]{1,0:T(8,128)(2,1)S(1)} %collective-permute-done.7.u4.refs_12_) | copy-start | bytes 1572868
  41.0 2.9 %collective-permute-start.11 = (bf16[128,2048]{1,0:T(8,128)(2,1)S(1)}, bf16[128,2048]{1,0:T(8,128)(2,1)S(1)}, u32[]{:S(2)}, u32[]{:S(2)}) collective-permute-start(bf16[128,2048]{1,0:T(8,128)(2,1)S(1)} %collective-permute-done.7.u4.refs_12_), channel_id=1, source_target_pairs={{0,8},{8,0},{1,9},{9,1},{2,10},{10,2},{3,11},{11,3},{4,12},{12,4},... | collective-permute-start | bytes 1572872 | tf_op jit(solution)/shard_map/ppermute | solution.py:31
  41.0 2.9 %collective-permute-start.12 = (bf16[128,2048]{1,0:T(8,128)(2,1)}, bf16[128,2048]{1,0:T(8,128)(2,1)S(1)}, u32[]{:S(2)}, u32[]{:S(2)}) collective-permute-start(bf16[128,2048]{1,0:T(8,128)(2,1)} %collective-permute-done.8.u5.refs_13_), channel_id=1, source_target_pairs={{0,8},{8,0},{1,9},{9,1},{2,10},{10,2},{3,11},{11,3},{4,12},{12,4},... | collective-permute-start | bytes 1572872 | tf_op jit(solution)/shard_map/ppermute | solution.py:31
  41.5 2.4 %copy-start.13 = (bf16[128,2048]{1,0:T(8,128)(2,1)}, bf16[128,2048]{1,0:T(8,128)(2,1)S(1)}, u32[]{:S(2)}) copy-start(bf16[128,2048]{1,0:T(8,128)(2,1)S(1)} %collective-permute-done.9.u2.refs_10_) | copy-start | bytes 1572868
  41.5 2.4 %copy-start.14 = (bf16[128,2048]{1,0:T(8,128)(2,1)}, bf16[128,2048]{1,0:T(8,128)(2,1)S(1)}, u32[]{:S(2)}) copy-start(bf16[128,2048]{1,0:T(8,128)(2,1)S(1)} %collective-permute-done.10.u3.refs_11_) | copy-start | bytes 1572868
  43.9 6.6 %copy-start.15 = (bf16[128,2048]{1,0:T(8,128)(2,1)}, bf16[128,2048]{1,0:T(8,128)(2,1)S(1)}, u32[]{:S(2)}) copy-start(bf16[128,2048]{1,0:T(8,128)(2,1)S(1)} %collective-permute-done.11.u6.refs_14_) | copy-start | bytes 1572868
  43.9 6.6 %copy-start.16 = (bf16[128,2048]{1,0:T(8,128)(2,1)}, bf16[128,2048]{1,0:T(8,128)(2,1)S(1)}, u32[]{:S(2)}) copy-start(bf16[128,2048]{1,0:T(8,128)(2,1)S(1)} %collective-permute-done.12.u7.refs_15_) | copy-start | bytes 1572868
  50.5 5.7 %collective-permute-start.13 = (f32[3,2048]{1,0:T(4,128)S(1)}, f32[3,2048]{1,0:T(4,128)S(1)}, u32[]{:S(2)}, u32[]{:S(2)}) collective-permute-start(f32[3,2048]{1,0:T(4,128)S(1)} %get-tuple-element.60.message), channel_id=1, source_target_pairs={{0,1},{1,0},{2,3},{3,2},{4,5},{5,4},{6,7},{7,6},{8,9},{9,8},{10,11... | collective-permute-start | bytes 73736 | tf_op jit(solution)/shard_map/ppermute | solution.py:528
  56.8 7.8 %collective-permute-start.16 = (f32[3,2048]{1,0:T(4,128)S(1)}, f32[3,2048]{1,0:T(4,128)S(1)}, u32[]{:S(2)}, u32[]{:S(2)}) collective-permute-start(f32[3,2048]{1,0:T(4,128)S(1)} %shard_map.114), channel_id=1, source_target_pairs={{0,2},{2,4},{4,6},{6,0},{1,3},{3,5},{5,7},{7,1},{8,10},{10,12},{12... | collective-permute-start | bytes 73736 | tf_op jit(solution)/shard_map/ppermute | solution.py:533
  60.0 6.1 %collective-permute-start.15 = (f32[3,2048]{1,0:T(4,128)S(1)}, f32[3,2048]{1,0:T(4,128)S(1)}, u32[]{:S(2)}, u32[]{:S(2)}) collective-permute-start(f32[3,2048]{1,0:T(4,128)S(1)} %shard_map.114), channel_id=1, source_target_pairs={{0,4},{2,6},{4,0},{6,2},{1,5},{3,7},{5,1},{7,3},{8,12},{10,14},{12... | collective-permute-start | bytes 73736 | tf_op jit(solution)/shard_map/ppermute | solution.py:533
  63.9 3.9 %collective-permute-start.14 = (f32[3,2048]{1,0:T(4,128)S(1)}, f32[3,2048]{1,0:T(4,128)S(1)}, u32[]{:S(2)}, u32[]{:S(2)}) collective-permute-start(f32[3,2048]{1,0:T(4,128)S(1)} %shard_map.114), channel_id=1, source_target_pairs={{0,6},{2,0},{4,2},{6,4},{1,7},{3,1},{5,3},{7,5},{8,14},{10,8},{12,... | collective-permute-start | bytes 73736 | tf_op jit(solution)/shard_map/ppermute | solution.py:533
  73.1 9.0 %copy-start.1 = (bf16[512,2048]{1,0:T(8,128)(2,1)}, bf16[512,2048]{1,0:T(8,128)(2,1)S(1)}, u32[]{:S(2)}) copy-start(bf16[512,2048]{1,0:T(8,128)(2,1)S(1)} %get-tuple-element.72.d_values_in.d) | copy-start | bytes 6291460
  73.1 9.0 %collective-permute-start.20 = (bf16[512,2048]{1,0:T(8,128)(2,1)}, bf16[512,2048]{1,0:T(8,128)(2,1)S(1)}, u32[]{:S(2)}, u32[]{:S(2)}) collective-permute-start(bf16[512,2048]{1,0:T(8,128)(2,1)} %get-tuple-element.75), channel_id=1, source_target_pairs={{0,8},{8,0},{1,9},{9,1},{2,10},{10,2},{3,11},{11,3},{4,12},{12,4},... | collective-permute-start | bytes 6291464 | tf_op jit(solution)/shard_map/ppermute | solution.py:31
  80.0 3.6 %copy-start = (bf16[512,1024]{1,0:T(8,128)(2,1)}, bf16[512,1024]{1,0:T(8,128)(2,1)S(1)}, u32[]{:S(2)}) copy-start(bf16[512,1024]{1,0:T(8,128)(2,1)S(1)} %get-tuple-element.70.d_query_in.d) | copy-start | bytes 3145732
  80.8 2.8 %collective-permute-start.19 = (bf16[512,1024]{1,0:T(8,128)(2,1)S(1)}, bf16[512,1024]{1,0:T(8,128)(2,1)S(1)}, u32[]{:S(2)}, u32[]{:S(2)}) collective-permute-start(bf16[512,1024]{1,0:T(8,128)(2,1)S(1)} %shard_map.118), channel_id=1, source_target_pairs={{0,8},{8,0},{1,9},{9,1},{2,10},{10,2},{3,11},{11,3},{4,12},{12,4},... | collective-permute-start | bytes 3145736 | tf_op jit(solution)/shard_map/ppermute | solution.py:31
  82.0 3.1 %collective-permute-start.18 = (bf16[512,1024]{1,0:T(8,128)(2,1)S(1)}, bf16[512,1024]{1,0:T(8,128)(2,1)S(1)}, u32[]{:S(2)}, u32[]{:S(2)}) collective-permute-start(bf16[512,1024]{1,0:T(8,128)(2,1)S(1)} %shard_map.119), channel_id=1, source_target_pairs={{0,8},{8,0},{1,9},{9,1},{2,10},{10,2},{3,11},{11,3},{4,12},{12,4},... | collective-permute-start | bytes 3145736 | tf_op jit(solution)/shard_map/ppermute | solution.py:31
  148.7 44.2 %all-to-all-start.1 = ((bf16[32,8,4096]{2,1,0:T(8,128)(2,1)}), bf16[32,8,4096]{2,1,0:T(8,128)(2,1)S(1)}, u32[]{:S(2)}, u32[]{:S(2)}) async-start(bf16[32,8,4096]{2,1,0:T(8,128)(2,1)} %shard_map.123), calls=%async_computation.1 | async-start | bytes 4194304 | tf_op jit(solution)/shard_map/all_to_all | solution.py:584
  154.6 26.3 %collective-permute-start.17 = (bf16[1,1024]{1,0:T(2,128)(2,1)S(1)}, bf16[1,1024]{1,0:T(2,128)(2,1)S(1)}, u32[]{:S(2)}, u32[]{:S(2)}) collective-permute-start(bf16[1,1024]{1,0:T(2,128)(2,1)S(1)} %slice.31), channel_id=1, source_target_pairs={{1,0},{2,1},{3,2},{4,3},{5,4},{6,5},{7,6},{9,8},{10,9},{11,10},{12... | collective-permute-start | bytes 6152 | tf_op jit(solution)/shard_map/ppermute | solution.py:35
